TPU v7x, 32 devices: a whole 2x2x4 slice. The times are simulated.
32 devices in a mesh: gx: 8 (over z, core), gy: 4 (over y, x).
Axes of the slice: x: 2, y: 2, z: 4, core: 2. Of those that a mesh axis runs over, the one named last changes fastest.
Arguments:
- points: bfloat16 [64, 65536], P(None, ('gx', 'gy')), may hold values from -6 to 6
- vectors: bfloat16 [32, 65536], P(None, ('gx', 'gy')), may hold values from -6 to 6
- leaf_pick: int32 [128, 128], P(('gx', 'gy')), may hold values from 0 to 511
- leaf_assign: int32 [128, 512], P(('gx', 'gy')), may hold values from 0 to 127
- device_pick: int32 [32, 128], P(('gx', 'gy')), may hold values from 0 to 511
- device_assign: int32 [32, 512], P(('gx', 'gy')), may hold values from 0 to 127
- node_pick: int32 [8, 3, 128], P('gx'), may hold values from 0 to 255
- node_assign: int32 [8, 3, 256], P('gx'), may hold values from 0 to 127
- far_mask: int32 [8, 8], P('gx'), may hold values from 0 to 1, as said below
- near_lower: int32 [32, 4, 12], P(('gx', 'gy')), may hold values from -1 to 3, as said below
- near_upper: int32 [32, 4, 12], P(('gx', 'gy')), may hold values from 0 to 3, as said below
Outputs:
- potential: float32 [32, 65536], P(None, ('gx', 'gy'))
Inputs may be any that keep to these rules, and one draw needn't show every extreme that they name: near_lower[d, o, j] is a local leaf of device d forming a near pair with local leaf near_upper[d, o, j] of device d + o + 1, or -1 for an empty slot; the slots of one d and o never name the same pair of leaves, and no live slot names a device past the last. `near_upper`: A local leaf of device d + o + 1, read only where near_lower is live. `far_mask`: Symmetric, zero on the diagonal, one where the two group indices differ by exactly 1.
All inputs are finite; a program needn't handle non-finite values.
Results may differ from a plain program's by a relative error of at most 0.0015.
Values may be sent and summed in bfloat16 or wider, within the bound.
No kernel may reach another device: no remote copies, remote signals or barrier semaphores. Data moves between devices by JAX's collectives and lax.ppermute only.
A program may use at most 128 MiB of HBM per device.

v0:
```python
import jax
import jax.numpy as jnp
from jax import lax
from jax.sharding import PartitionSpec as P

DIM = 64
COLS = 32
LEAF = 512
SKEL = 128
LPD = 4


KERNEL_RATE = 2.0


def passed_along(value, axis, steps):
    count = lax.axis_size(axis)
    first, last = (max(0, -steps), min(count, count - steps))
    return lax.ppermute(value, axis, [(source, source + steps) for source in range(first, last)])


def from_partner(value, axis, bit):
    mask = 2**bit
    pairs = [(source, source ^ mask) for source in range(lax.axis_size(axis))]
    return lax.ppermute(value, axis, pairs)


def kernel_block(source, target):
    decay_rate = KERNEL_RATE / source.shape[0]
    source_wide = source.astype(jnp.float32)
    target_wide = target.astype(jnp.float32)
    source_norm = jnp.sum(source_wide * source_wide, axis=0)
    target_norm = jnp.sum(target_wide * target_wide, axis=0)
    products = lax.dot_general(
        source, target, (((0,), (0,)), ((), ())), preferred_element_type=jnp.float32
    )
    return jnp.exp(-decay_rate * (source_norm[:, None] + target_norm[None, :] - 2.0 * products))


def add_columns(running, terms, first_col):
    current = lax.dynamic_slice_in_dim(running, first_col, terms.shape[1], 1)
    return lax.dynamic_update_slice_in_dim(running, current + terms, first_col, 1)


def pick_columns(table_matrix, col_index):
    return jnp.take(table_matrix, col_index, axis=1)


def one_hot(assignment, width_count):
    return (assignment[:, None] == jnp.arange(width_count, dtype=jnp.int32)[None, :]).astype(
        jnp.float32
    )


def pair_terms(low_points, low_values, high_points, high_values):
    kernel_tile = kernel_block(low_points, high_points).astype(jnp.bfloat16)
    to_upper = jnp.dot(low_values, kernel_tile, preferred_element_type=jnp.float32)
    to_lower = lax.dot_general(
        high_values, kernel_tile, (((1,), (1,)), ((), ())), preferred_element_type=jnp.float32
    )
    return (to_lower, to_upper)


def neighbour_terms(
    offset,
    near_lower,
    near_upper,
    points,
    columns,
    high_block,
    high_columns,
    near_terms,
    upper_terms,
):
    for slot_index in range(near_lower.shape[2]):
        lower_leaf = near_lower[0, offset - 1, slot_index]
        upper_leaf = near_upper[0, offset - 1, slot_index]
        live_flag = lower_leaf >= 0
        lower_col = jnp.maximum(lower_leaf, 0) * LEAF
        upper_col = upper_leaf * LEAF
        low_points = lax.dynamic_slice_in_dim(points, lower_col, LEAF, 1)
        low_values = lax.dynamic_slice_in_dim(columns, lower_col, LEAF, 1)
        high_points = lax.dynamic_slice_in_dim(high_block, upper_col, LEAF, 1)
        high_values = lax.dynamic_slice_in_dim(high_columns, upper_col, LEAF, 1)
        to_lower, to_upper = pair_terms(low_points, low_values, high_points, high_values)
        live_scale = live_flag.astype(jnp.float32)
        to_lower = to_lower * live_scale
        to_upper = to_upper * live_scale
        near_terms = add_columns(near_terms, to_lower, lower_col)
        upper_terms = add_columns(upper_terms, to_upper, upper_col)
    return (near_terms, upper_terms)


def on_device(
    points,
    vectors,
    leaf_pick,
    leaf_assign,
    device_pick,
    device_assign,
    node_pick,
    node_assign,
    far_mask,
    near_lower,
    near_upper,
):
    device_cols = points.shape[1]
    reach_count = lax.axis_size("gy")
    levels = reach_count.bit_length() - 1
    row_index = lax.axis_index("gy")

    def self_target(target, running):
        first_col = target * LEAF
        target_points = lax.dynamic_slice_in_dim(points, first_col, LEAF, 1)
        kernel_tile = kernel_block(points, target_points).astype(jnp.bfloat16)
        self_terms = jnp.dot(vectors, kernel_tile, preferred_element_type=jnp.float32)
        return lax.dynamic_update_slice_in_dim(running, self_terms, first_col, 1)

    near_terms = lax.fori_loop(0, LPD, self_target, jnp.zeros((COLS, device_cols), jnp.float32))
    for offset in range(1, reach_count + 1):
        high_block, high_columns = passed_along((points, vectors), ("gx", "gy"), -offset)
        upper_terms = jnp.zeros((COLS, device_cols), jnp.float32)
        near_terms, upper_terms = neighbour_terms(
            offset,
            near_lower,
            near_upper,
            points,
            vectors,
            high_block,
            high_columns,
            near_terms,
            upper_terms,
        )
        near_terms = near_terms + passed_along(upper_terms, ("gx", "gy"), offset)
    leaf_points = points.reshape(DIM, LPD, LEAF)
    leaf_values = vectors.reshape(COLS, LPD, LEAF)
    skeleton_points = jax.vmap(pick_columns, in_axes=(1, 0))(leaf_points, leaf_pick)
    leaf_onehot = leaf_assign[:, :, None] == jnp.arange(SKEL, dtype=jnp.int32)[None, None, :]
    leaf_weights = jnp.einsum(
        "cln,lns->lcs",
        leaf_values,
        leaf_onehot.astype(jnp.bfloat16),
        preferred_element_type=jnp.float32,
    )
    joined_points = skeleton_points.transpose(1, 0, 2).reshape(DIM, LPD * SKEL)
    joined_weights = leaf_weights.transpose(1, 0, 2).reshape(COLS, LPD * SKEL)
    node_points = jnp.take(joined_points, device_pick[0], axis=1)
    device_onehot = one_hot(device_assign[0], SKEL)
    node_weights = jnp.dot(joined_weights, device_onehot, precision=lax.Precision.HIGHEST)
    path_onehots = []
    for level_index in range(1, levels + 1):
        heap_index = (reach_count >> level_index) - 1 + (row_index >> level_index)
        assignment = lax.dynamic_index_in_dim(node_assign[0], heap_index, 0, keepdims=False)
        path_onehots.append(one_hot(assignment, SKEL))
    for level_index in range(1, levels + 1):
        bit_index = level_index - 1
        other_points = from_partner(node_points, "gy", bit_index)
        other_weights = from_partner(node_weights, "gy", bit_index)
        upper_side = row_index >> bit_index & 1 == 1
        pair_points = jnp.where(
            upper_side,
            jnp.concatenate([other_points, node_points], 1),
            jnp.concatenate([node_points, other_points], 1),
        )
        pair_weights = jnp.where(
            upper_side,
            jnp.concatenate([other_weights, node_weights], 1),
            jnp.concatenate([node_weights, other_weights], 1),
        )
        heap_index = (reach_count >> level_index) - 1 + (row_index >> level_index)
        node_picks = lax.dynamic_index_in_dim(node_pick[0], heap_index, 0, keepdims=False)
        node_points = jnp.take(pair_points, node_picks, axis=1)
        node_weights = jnp.dot(
            pair_weights, path_onehots[level_index - 1], precision=lax.Precision.HIGHEST
        )
    gathered_roots = lax.all_gather(node_points[None], "gx", axis=0, tiled=True)
    far_flags = far_mask[0].astype(jnp.float32)
    root_kernels = jax.vmap(kernel_block, in_axes=(0, None))(gathered_roots, node_points)
    node_potential = jnp.einsum(
        "n,ncs,nst->ct",
        far_flags,
        lax.all_gather(node_weights[None], "gx", axis=0, tiled=True),
        root_kernels,
        precision=lax.Precision.HIGHEST,
    )
    for level_index in range(levels, 0, -1):
        child_potential = jnp.dot(
            node_potential, path_onehots[level_index - 1].T, precision=lax.Precision.HIGHEST
        )
        child_side = row_index >> level_index - 1 & 1
        node_potential = lax.dynamic_slice_in_dim(child_potential, child_side * SKEL, SKEL, 1)
    leaf_joined = jnp.dot(node_potential, device_onehot.T, precision=lax.Precision.HIGHEST).reshape(
        COLS, LPD, SKEL
    )
    far_terms = jnp.einsum(
        "cls,lns->cln",
        leaf_joined,
        leaf_onehot.astype(jnp.float32),
        precision=lax.Precision.HIGHEST,
    ).reshape(COLS, device_cols)
    return near_terms + far_terms


def solution(mesh):
    placed = (
        P(None, ("gx", "gy")),
        P(None, ("gx", "gy")),
        P(("gx", "gy"), None),
        P(("gx", "gy"), None),
        P(("gx", "gy"), None),
        P(("gx", "gy"), None),
        P("gx", None, None),
        P("gx", None, None),
        P("gx", None),
        P(("gx", "gy"), None, None),
        P(("gx", "gy"), None, None),
    )
    return jax.shard_map(
        on_device, mesh=mesh, in_specs=placed, out_specs=P(None, ("gx", "gy")), check_vma=False
    )
```

profile of v0, /device:TPU:5, one launch (start us, length us, event | category | flops | bytes accessed | tf_op | source)
XLA Modules:
  0.0 233.5 jit_solution(3398589110747293190)
XLA Ops:
  0.0 3.2 %collective-permute-start.1 = (bf16[64,2048]{1,0:T(8,128)(2,1)}, bf16[64,2048]{1,0:T(8,128)(2,1)S(1)}, u32[]{:S(2)}, u32[]{:S(2)}) collective-permute-start(bf16[64,2048]{1,0:T(8,128)(2,1)} %param.15), channel_id=1, source_target_pairs={{1,0},{2,1},{3,2},{4,3},{5,4},{6,5},{7,6},{8,7},{9,8},{10,9},{11,1... | collective-permute-start | bytes 786440 | tf_op jit(solution)/shard_map/ppermute | solution.py:19
  3.2 3.7 %collective-permute-start.4 = (bf16[64,2048]{1,0:T(8,128)(2,1)}, bf16[64,2048]{1,0:T(8,128)(2,1)S(1)}, u32[]{:S(2)}, u32[]{:S(2)}) collective-permute-start(bf16[64,2048]{1,0:T(8,128)(2,1)} %param.15), channel_id=1, source_target_pairs={{2,0},{3,1},{4,2},{5,3},{6,4},{7,5},{8,6},{9,7},{10,8},{11,9},{12,... | collective-permute-start | bytes 786440 | tf_op jit(solution)/shard_map/ppermute | solution.py:19
  6.9 2.4 %collective-permute-start = (bf16[32,2048]{1,0:T(8,128)(2,1)}, bf16[32,2048]{1,0:T(8,128)(2,1)S(1)}, u32[]{:S(2)}, u32[]{:S(2)}) collective-permute-start(bf16[32,2048]{1,0:T(8,128)(2,1)} %param.16), channel_id=1, source_target_pairs={{1,0},{2,1},{3,2},{4,3},{5,4},{6,5},{7,6},{8,7},{9,8},{10,9},{11,1... | collective-permute-start | bytes 393224 | tf_op jit(solution)/shard_map/ppermute | solution.py:19
  9.4 1.9 collective-permute-start.3
  11.3 1.2 copy.24
  12.7 3.2 %gather_fusion.1 = bf16[512,64]{1,0:T(8,128)(2,1)S(1)} fusion(bf16[4,64,512]{1,2,0:T(8,128)(2,1)S(1)} %bitcast.341, s32[512]{0:T(512)S(1)} %fusion.383), kind=kCustom, calls=%fused_computation.3 | custom fusion | bytes 135168 | tf_op jit(solution)/shard_map/vmap(jit(_take))/gather | solution.py:46
  16.8 1.5 collective-permute-start.14
  112.8 6.5 %while.13 = (s32[]{:T(128)}, f32[32,2048]{1,0:T(8,128)S(1)}, bf16[64,2048]{1,0:T(8,128)(2,1)S(1)}, bf16[32,2048]{1,0:T(8,128)(2,1)S(1)}, s32[]{:T(128)}, /*index=5*/s32[]{:T(128)}, s32[]{:T(128)}, s32[]{:T(128)}) while((s32[]{:T(128)}, f32[32,2048]{1,0:T(8,128)S(1)}, bf16[64,2048]{1,0:T(8,128)(2,1)S(1)}, bf16[32,2048]{1,0:T(8,128)(2,1)S(1)}, ...), condition=%wide.region_3.0_spmd, body=%wide.region_0.0_spmd.sunk | while | flops 207058432 | bytes 873615 | solution.py:119
  113.0 1.5 fusion.505
  114.6 1.5 fusion.505
  116.2 1.5 fusion.505
  117.9 1.5 fusion.505
  123.1 1.7 collective-permute-done.12
  125.3 2.2 collective-permute-done.15
  129.3 17.5 %all-gather.1 = bf16[512,128]{1,0:T(8,128)(2,1)S(1)} all-gather(bf16[64,128]{1,0:T(8,128)(2,1)S(1)} %copy.25), channel_id=3, replica_groups=mesh['gx'=8,'gy'=4] {'gx'}, dimensions={0}, use_global_device_ids=true | all-gather | bytes 147456 | tf_op jit(solution)/shard_map/all_gather | solution.py:176
  146.8 2.6 %collective-permute-start.7 = (bf16[64,2048]{1,0:T(8,128)(2,1)S(1)}, bf16[64,2048]{1,0:T(8,128)(2,1)S(1)}, u32[]{:S(2)}, u32[]{:S(2)}) collective-permute-start(bf16[64,2048]{1,0:T(8,128)(2,1)S(1)} %get-tuple-element.348), channel_id=1, source_target_pairs={{3,0},{4,1},{5,2},{6,3},{7,4},{8,5},{9,6},{10,7},{11,8},{12,9},{13... | collective-permute-start | bytes 786440 | tf_op jit(solution)/shard_map/ppermute | solution.py:19
  149.7 14.9 %all-gather = f32[256,128]{1,0:T(8,128)S(1)} all-gather(f32[32,128]{1,0:T(8,128)S(1)} %fusion.308), channel_id=2, replica_groups=mesh['gx'=8,'gy'=4] {'gx'}, dimensions={0}, use_global_device_ids=true | all-gather | bytes 147456 | tf_op jit(solution)/shard_map/all_gather | solution.py:182
  167.4 2.3 collective-permute-start.6
  177.4 1.9 collective-permute-start.10
  187.1 2.1 collective-permute-start.9
  197.0 3.5 %collective-permute-start.2 = (f32[32,2048]{1,0:T(8,128)S(1)}, f32[32,2048]{1,0:T(8,128)S(1)}, u32[]{:S(2)}, u32[]{:S(2)}) collective-permute-start(f32[32,2048]{1,0:T(8,128)S(1)} %fusion.234), channel_id=1, source_target_pairs={{0,1},{1,2},{2,3},{3,4},{4,5},{5,6},{6,7},{7,8},{8,9},{9,10},{10,1... | collective-permute-start | bytes 786440 | tf_op jit(solution)/shard_map/ppermute | solution.py:19
  208.4 4.5 %collective-permute-start.5 = (f32[32,2048]{1,0:T(8,128)S(1)}, f32[32,2048]{1,0:T(8,128)S(1)}, u32[]{:S(2)}, u32[]{:S(2)}) collective-permute-start(f32[32,2048]{1,0:T(8,128)S(1)} %fusion.256), channel_id=1, source_target_pairs={{0,2},{1,3},{2,4},{3,5},{4,6},{5,7},{6,8},{7,9},{8,10},{9,11},{10,... | collective-permute-start | bytes 786440 | tf_op jit(solution)/shard_map/ppermute | solution.py:19
  216.1 3.4 %collective-permute-start.8 = (f32[32,2048]{1,0:T(8,128)S(1)}, f32[32,2048]{1,0:T(8,128)S(1)}, u32[]{:S(2)}, u32[]{:S(2)}) collective-permute-start(f32[32,2048]{1,0:T(8,128)S(1)} %fusion.278), channel_id=1, source_target_pairs={{0,3},{1,4},{2,5},{3,6},{4,7},{5,8},{6,9},{7,10},{8,11},{9,12},{10... | collective-permute-start | bytes 786440 | tf_op jit(solution)/shard_map/ppermute | solution.py:19
  219.6 3.3 %collective-permute-start.11 = (f32[32,2048]{1,0:T(8,128)S(1)}, f32[32,2048]{1,0:T(8,128)S(1)}, u32[]{:S(2)}, u32[]{:S(2)}) collective-permute-start(f32[32,2048]{1,0:T(8,128)S(1)} %fusion.300), channel_id=1, source_target_pairs={{0,4},{1,5},{2,6},{3,7},{4,8},{5,9},{6,10},{7,11},{8,12},{9,13},{1... | collective-permute-start | bytes 786440 | tf_op jit(solution)/shard_map/ppermute | solution.py:19
  (244 shorter events, 57.6 us)
Async XLA Ops:
  0.0 12.6 %copy-start.4 = (s32[4,128]{1,0:T(4,128)S(1)}, s32[4,128]{1,0:T(4,128)}, u32[]{:S(2)}) copy-start(s32[4,128]{1,0:T(4,128)} %param.17) | copy-start | bytes 6148
  0.0 12.6 %copy-start.8 = (s32[1,128]{1,0:T(1,128)S(1)}, s32[1,128]{1,0:T(1,128)}, u32[]{:S(2)}) copy-start(s32[1,128]{1,0:T(1,128)} %param.19) | copy-start | bytes 1540
  0.0 167.4 %collective-permute-start.1 = (bf16[64,2048]{1,0:T(8,128)(2,1)}, bf16[64,2048]{1,0:T(8,128)(2,1)S(1)}, u32[]{:S(2)}, u32[]{:S(2)}) collective-permute-start(bf16[64,2048]{1,0:T(8,128)(2,1)} %param.15), channel_id=1, source_target_pairs={{1,0},{2,1},{3,2},{4,3},{5,4},{6,5},{7,6},{8,7},{9,8},{10,9},{11,1... | collective-permute-start | bytes 786440 | tf_op jit(solution)/shard_map/ppermute | solution.py:19
  3.2 174.2 %collective-permute-start.4 = (bf16[64,2048]{1,0:T(8,128)(2,1)}, bf16[64,2048]{1,0:T(8,128)(2,1)S(1)}, u32[]{:S(2)}, u32[]{:S(2)}) collective-permute-start(bf16[64,2048]{1,0:T(8,128)(2,1)} %param.15), channel_id=1, source_target_pairs={{2,0},{3,1},{4,2},{5,3},{6,4},{7,5},{8,6},{9,7},{10,8},{11,9},{12,... | collective-permute-start | bytes 786440 | tf_op jit(solution)/shard_map/ppermute | solution.py:19
  6.9 201.4 %collective-permute-start = (bf16[32,2048]{1,0:T(8,128)(2,1)}, bf16[32,2048]{1,0:T(8,128)(2,1)S(1)}, u32[]{:S(2)}, u32[]{:S(2)}) collective-permute-start(bf16[32,2048]{1,0:T(8,128)(2,1)} %param.16), channel_id=1, source_target_pairs={{1,0},{2,1},{3,2},{4,3},{5,4},{6,5},{7,6},{8,7},{9,8},{10,9},{11,1... | collective-permute-start | bytes 393224 | tf_op jit(solution)/shard_map/ppermute | solution.py:19
  9.4 210.2 %collective-permute-start.3 = (bf16[32,2048]{1,0:T(8,128)(2,1)}, bf16[32,2048]{1,0:T(8,128)(2,1)S(1)}, u32[]{:S(2)}, u32[]{:S(2)}) collective-permute-start(bf16[32,2048]{1,0:T(8,128)(2,1)} %param.16), channel_id=1, source_target_pairs={{2,0},{3,1},{4,2},{5,3},{6,4},{7,5},{8,6},{9,7},{10,8},{11,9},{12,... | collective-permute-start | bytes 393224 | tf_op jit(solution)/shard_map/ppermute | solution.py:19
  12.7 6.9 %copy-start.3 = (s32[1,4,12]{2,1,0:T(4,128)S(1)}, s32[1,4,12]{2,1,0:T(4,128)}, u32[]{:S(2)}) copy-start(s32[1,4,12]{2,1,0:T(4,128)} %param.25) | copy-start | bytes 580
  16.8 105.3 %collective-permute-start.14 = (bf16[64,128]{0,1:T(8,128)(2,1)S(1)}, bf16[64,128]{0,1:T(8,128)(2,1)S(1)}, u32[]{:S(2)}, u32[]{:S(2)}) collective-permute-start(bf16[64,128]{0,1:T(8,128)(2,1)S(1)} %select_bitcast_fusion.1), channel_id=1, source_target_pairs={{0,1},{1,0},{2,3},{3,2},{4,5},{5,4},{6,7},{7,6},{8,9},{9,8},{10,11... | collective-permute-start | bytes 49160 | tf_op jit(solution)/shard_map/ppermute | solution.py:25
  28.6 84.1 %copy-start.6 = (s32[1,3,256]{2,0,1:T(1,128)S(1)}, s32[1,3,256]{2,0,1:T(1,128)}, u32[]{:S(2)}) copy-start(s32[1,3,256]{2,0,1:T(1,128)} %param.22) | copy-start | bytes 9220
  29.4 83.4 %copy-start.10 = (s32[1,8]{1,0:T(1,128)S(1)}, s32[1,8]{1,0:T(1,128)}, u32[]{:S(2)}) copy-start(s32[1,8]{1,0:T(1,128)} %param.23) | copy-start | bytes 100
  50.6 62.2 %copy-start = (bf16[64,2048]{1,0:T(8,128)(2,1)S(1)}, bf16[64,2048]{1,0:T(8,128)(2,1)}, u32[]{:S(2)}) copy-start(bf16[64,2048]{1,0:T(8,128)(2,1)} %param.15) | copy-start | bytes 786436
  50.6 62.2 %copy-start.1 = (bf16[32,2048]{1,0:T(8,128)(2,1)S(1)}, bf16[32,2048]{1,0:T(8,128)(2,1)}, u32[]{:S(2)}) copy-start(bf16[32,2048]{1,0:T(8,128)(2,1)} %param.16) | copy-start | bytes 393220
  112.8 6.7 %copy-start.9 = (s32[4,512]{1,0:T(4,128)S(1)}, s32[4,512]{1,0:T(4,128)}, u32[]{:S(2)}) copy-start(s32[4,512]{1,0:T(4,128)} %param.18) | copy-start | bytes 24580
  122.2 2.7 %collective-permute-start.12 = (f32[32,128]{1,0:T(8,128)S(1)}, f32[32,128]{1,0:T(8,128)S(1)}, u32[]{:S(2)}, u32[]{:S(2)}) collective-permute-start(f32[32,128]{1,0:T(8,128)S(1)} %fusion.303), channel_id=1, source_target_pairs={{0,1},{1,0},{2,3},{3,2},{4,5},{5,4},{6,7},{7,6},{8,9},{9,8},{10,11... | collective-permute-start | bytes 49160 | tf_op jit(solution)/shard_map/ppermute | solution.py:25
  124.8 2.8 %collective-permute-start.15 = (bf16[64,128]{0,1:T(8,128)(2,1)S(1)}, bf16[64,128]{0,1:T(8,128)(2,1)S(1)}, u32[]{:S(2)}, u32[]{:S(2)}) collective-permute-start(bf16[64,128]{0,1:T(8,128)(2,1)S(1)} %select_bitcast_fusion), channel_id=1, source_target_pairs={{0,2},{1,3},{2,0},{3,1},{4,6},{5,7},{6,4},{7,5},{8,10},{9,11},{10,... | collective-permute-start | bytes 49160 | tf_op jit(solution)/shard_map/ppermute | solution.py:25
  127.6 19.3 %collective-permute-start.13 = (f32[32,128]{1,0:T(8,128)S(1)}, f32[32,128]{1,0:T(8,128)S(1)}, u32[]{:S(2)}, u32[]{:S(2)}) collective-permute-start(f32[32,128]{1,0:T(8,128)S(1)} %fusion.310), channel_id=1, source_target_pairs={{0,2},{1,3},{2,0},{3,1},{4,6},{5,7},{6,4},{7,5},{8,10},{9,11},{10,... | collective-permute-start | bytes 49160 | tf_op jit(solution)/shard_map/ppermute | solution.py:25
  146.8 40.3 %collective-permute-start.7 = (bf16[64,2048]{1,0:T(8,128)(2,1)S(1)}, bf16[64,2048]{1,0:T(8,128)(2,1)S(1)}, u32[]{:S(2)}, u32[]{:S(2)}) collective-permute-start(bf16[64,2048]{1,0:T(8,128)(2,1)S(1)} %get-tuple-element.348), channel_id=1, source_target_pairs={{3,0},{4,1},{5,2},{6,3},{7,4},{8,5},{9,6},{10,7},{11,8},{12,9},{13... | collective-permute-start | bytes 786440 | tf_op jit(solution)/shard_map/ppermute | solution.py:19
  167.4 58.8 %collective-permute-start.6 = (bf16[32,2048]{1,0:T(8,128)(2,1)S(1)}, bf16[32,2048]{1,0:T(8,128)(2,1)S(1)}, u32[]{:S(2)}, u32[]{:S(2)}) collective-permute-start(bf16[32,2048]{1,0:T(8,128)(2,1)S(1)} %get-tuple-element.353), channel_id=1, source_target_pairs={{3,0},{4,1},{5,2},{6,3},{7,4},{8,5},{9,6},{10,7},{11,8},{12,9},{13... | collective-permute-start | bytes 393224 | tf_op jit(solution)/shard_map/ppermute | solution.py:19
  177.4 19.6 %collective-permute-start.10 = (bf16[64,2048]{1,0:T(8,128)(2,1)S(1)}, bf16[64,2048]{1,0:T(8,128)(2,1)S(1)}, u32[]{:S(2)}, u32[]{:S(2)}) collective-permute-start(bf16[64,2048]{1,0:T(8,128)(2,1)S(1)} %get-tuple-element.348), channel_id=1, source_target_pairs={{4,0},{5,1},{6,2},{7,3},{8,4},{9,5},{10,6},{11,7},{12,8},{13,9},{1... | collective-permute-start | bytes 786440 | tf_op jit(solution)/shard_map/ppermute | solution.py:19
  187.1 42.4 %collective-permute-start.9 = (bf16[32,2048]{1,0:T(8,128)(2,1)S(1)}, bf16[32,2048]{1,0:T(8,128)(2,1)S(1)}, u32[]{:S(2)}, u32[]{:S(2)}) collective-permute-start(bf16[32,2048]{1,0:T(8,128)(2,1)S(1)} %get-tuple-element.353), channel_id=1, source_target_pairs={{4,0},{5,1},{6,2},{7,3},{8,4},{9,5},{10,6},{11,7},{12,8},{13,9},{1... | collective-permute-start | bytes 393224 | tf_op jit(solution)/shard_map/ppermute | solution.py:19
  197.0 19.1 %collective-permute-start.2 = (f32[32,2048]{1,0:T(8,128)S(1)}, f32[32,2048]{1,0:T(8,128)S(1)}, u32[]{:S(2)}, u32[]{:S(2)}) collective-permute-start(f32[32,2048]{1,0:T(8,128)S(1)} %fusion.234), channel_id=1, source_target_pairs={{0,1},{1,2},{2,3},{3,4},{4,5},{5,6},{6,7},{7,8},{8,9},{9,10},{10,1... | collective-permute-start | bytes 786440 | tf_op jit(solution)/shard_map/ppermute | solution.py:19
  208.4 17.8 %collective-permute-start.5 = (f32[32,2048]{1,0:T(8,128)S(1)}, f32[32,2048]{1,0:T(8,128)S(1)}, u32[]{:S(2)}, u32[]{:S(2)}) collective-permute-start(f32[32,2048]{1,0:T(8,128)S(1)} %fusion.256), channel_id=1, source_target_pairs={{0,2},{1,3},{2,4},{3,5},{4,6},{5,7},{6,8},{7,9},{8,10},{9,11},{10,... | collective-permute-start | bytes 786440 | tf_op jit(solution)/shard_map/ppermute | solution.py:19
  216.1 13.3 %collective-permute-start.8 = (f32[32,2048]{1,0:T(8,128)S(1)}, f32[32,2048]{1,0:T(8,128)S(1)}, u32[]{:S(2)}, u32[]{:S(2)}) collective-permute-start(f32[32,2048]{1,0:T(8,128)S(1)} %fusion.278), channel_id=1, source_target_pairs={{0,3},{1,4},{2,5},{3,6},{4,7},{5,8},{6,9},{7,10},{8,11},{9,12},{10... | collective-permute-start | bytes 786440 | tf_op jit(solution)/shard_map/ppermute | solution.py:19
  219.6 13.1 %collective-permute-start.11 = (f32[32,2048]{1,0:T(8,128)S(1)}, f32[32,2048]{1,0:T(8,128)S(1)}, u32[]{:S(2)}, u32[]{:S(2)}) collective-permute-start(f32[32,2048]{1,0:T(8,128)S(1)} %fusion.300), channel_id=1, source_target_pairs={{0,4},{1,5},{2,6},{3,7},{4,8},{5,9},{6,10},{7,11},{8,12},{9,13},{1... | collective-permute-start | bytes 786440 | tf_op jit(solution)/shard_map/ppermute | solution.py:19
  (3 other events, 10.7 us)
where the time goes:
time: 235 us; the launch traced here: 233 us
  between operations  92.5 us (39%)
  matrix products  51.8 us (22%)
  starting transfers between devices  37.5 us (16%)
  blocking collectives  32.5 us (14%)
  local copies, waits for them, and re-layouts  11.1 us (5%)
  waiting for transfers between devices  4.06 us (2%)
  other arithmetic  3.96 us (2%)
    ppermute x12, starting transfers between devices, passed_along(): lax.ppermute(value, axis, [(source, source + steps) for source in range(f...  34.9 us
    dot_general x49, matrix products, kernel_block(): lax.dot_general(source, target, (((0,), (0,)), ((), ())), preferred_eleme...  20.8 us
    all_gather x1, blocking collectives, on_device(): gathered_roots = lax.all_gather(node_points[None], 'gx', axis=0, tiled=True)  17.5 us
    all_gather x1, blocking collectives, on_device(): lax.all_gather(node_weights[None], 'gx', axis=0, tiled=True)  14.9 us
    dot_general x48, matrix products, pair_terms(): lax.dot_general(high_values, kernel_tile, (((1,), (1,)), ((), ())), prefe...  12.2 us
    dot_general x48, matrix products, pair_terms(): jnp.dot(low_values, kernel_tile, preferred_element_type=jnp.float32)  9.1 us
    dot_general x4, matrix products, self_target(): jnp.dot(vectors, kernel_tile, preferred_element_type=jnp.float32)  6.01 us
  transfers between devices with their start and end apart: 16, of which 2 were waited for; matrix products, arithmetic and copies ran while one was open for 28% of the time, Pallas kernels for 0%

commit v1 on v0

v1 whole, which is shorter than its diff:
```python
import functools
import math

import jax
import jax.numpy as jnp
from jax import lax
from jax.experimental import pallas as pl
from jax.experimental.pallas import tpu as pltpu
from jax.sharding import PartitionSpec as P

LPD = 4
SKEL = 128
KERNEL_RATE = 2.0
LOG2E = math.log2(math.e)
ROWS_AUG = 16
F32, BF16 = jnp.float32, jnp.bfloat16
VMEM = pl.BlockSpec(memory_space=pltpu.VMEM)
SMEM = pl.BlockSpec(memory_space=pltpu.SMEM)


def passed_along(value, axis, steps):
    count = lax.axis_size(axis)
    first, last = (max(0, -steps), min(count, count - steps))
    return lax.ppermute(value, axis, [(source, source + steps) for source in range(first, last)])


def swapped(value, axis, mask):
    pairs = [(source, source ^ mask) for source in range(lax.axis_size(axis))]
    return lax.ppermute(value, axis, pairs)


def split3(value):
    first = value.astype(BF16)
    rest = value - first.astype(F32)
    second = rest.astype(BF16)
    third = (rest - second.astype(F32)).astype(BF16)
    return first, second, third


def norm_rows(points, scale, norms_first):
    wide = points.astype(F32)
    norm = -0.5 * scale * jnp.sum(wide * wide, axis=0, keepdims=True)
    row = lax.broadcasted_iota(jnp.int32, (ROWS_AUG, points.shape[1]), 0)
    start = 0 if norms_first else 3
    ones = (row >= 3 - start) & (row < 6 - start)
    rows = jnp.where(ones, 1.0, 0.0)
    for index, part in enumerate(split3(norm)):
        rows = jnp.where(row == start + index, part.astype(F32), rows)
    return rows.astype(BF16)


def source_rows(points, scale):
    parts = split3(points.astype(F32) * scale)
    return jnp.concatenate([*parts, norm_rows(points, scale, True)], 0).T


def target_columns(points, norms):
    return jnp.concatenate([points, points, points, norms], 0)


def tile_of(rows, points, norms):
    product = jnp.dot(rows, target_columns(points, norms), preferred_element_type=F32)
    return jnp.exp2(product).astype(BF16)


def dot_back(values, tile):
    return lax.dot_general(values, tile, (((1,), (1,)), ((), ())), preferred_element_type=F32)


def self_kernel(scale, leaf, points_ref, values_ref, rows_ref, near_ref, norms_ref, tiles_ref):
    norms_ref[...] = norm_rows(points_ref[...], scale, False)
    at = [pl.ds(index * leaf, leaf) for index in range(LPD)]
    for index in range(LPD):
        rows_ref[at[index], :] = source_rows(points_ref[:, at[index]], scale)
    near_ref[...] = jnp.zeros_like(near_ref)

    def add(slot, low, high):
        near_ref[:, at[high]] += jnp.dot(
            values_ref[:, at[low]], tiles_ref[slot], preferred_element_type=F32
        )
        if low != high:
            near_ref[:, at[low]] += dot_back(values_ref[:, at[high]], tiles_ref[slot])

    pairs = [(low, high) for low in range(LPD) for high in range(low, LPD)]
    for slot, (low, high) in enumerate(pairs):
        tiles_ref[slot] = tile_of(
            rows_ref[at[low], :], points_ref[:, at[high]], norms_ref[:, at[high]]
        )
        if slot:
            add(slot - 1, *pairs[slot - 1])
    add(len(pairs) - 1, *pairs[-1])


def pair_kernel(
    scale,
    leaf,
    offset,
    group,
    lower_ref,
    upper_ref,
    rows_ref,
    values_ref,
    other_ref,
    near_in,
    near_ref,
    out_ref,
    norms_ref,
    upper_sum,
    tiles_ref,
):
    dim = other_ref.shape[0] - values_ref.shape[0]
    near_ref[...] = near_in[...]
    upper_sum[...] = jnp.zeros_like(upper_sum)
    norms_ref[...] = norm_rows(other_ref[:dim, :], scale, False)

    def slot_of(index):
        low = lower_ref[0, offset, index]
        start = pl.multiple_of(jnp.maximum(low, 0) * leaf, leaf)
        return low >= 0, start, pl.multiple_of(upper_ref[0, offset, index] * leaf, leaf)

    def add(slot, live, low, high):
        flag = jnp.where(live, 1.0, 0.0).astype(BF16)
        low_at, high_at = pl.ds(low, leaf), pl.ds(high, leaf)
        tile = tiles_ref[slot]
        upper_sum[:, high_at] += jnp.dot(
            values_ref[:, low_at] * flag, tile, preferred_element_type=F32
        )
        near_ref[:, low_at] += dot_back(other_ref[dim:, high_at] * flag, tile)

    @pl.loop(0, lower_ref.shape[2] // group)
    def _(step):
        slots = [slot_of(step * group + index) for index in range(group)]
        some = functools.reduce(jnp.logical_or, [slot[0] for slot in slots])

        @pl.when(some)
        def _():
            for index, (_, low, high) in enumerate(slots):
                tiles_ref[index] = tile_of(
                    rows_ref[pl.ds(low, leaf), :],
                    other_ref[:dim, pl.ds(high, leaf)],
                    norms_ref[:, pl.ds(high, leaf)],
                )
                if index:
                    add(index - 1, *slots[index - 1])
            add(group - 1, *slots[group - 1])

    out_ref[...] = upper_sum[...].astype(BF16)


def picked(index_row, count):
    wide = (count, index_row.shape[1])
    rows = lax.broadcasted_iota(jnp.int32, wide, 0)
    return jnp.where(rows == index_row, 1.0, 0.0).astype(BF16)


def flags_dot(left, right):
    return jnp.dot(left, right, preferred_element_type=F32).astype(BF16)


def rise_kernel(
    levels,
    leaf,
    where_ref,
    points_ref,
    values_ref,
    leaf_pick,
    leaf_assign,
    device_pick,
    device_assign,
    node_pick,
    node_assign,
    share_ref,
    spread_ref,
):
    row_index = where_ref[1]
    picks = picked(device_pick[...], LPD * SKEL)
    assigns = picked(device_assign[...], SKEL)
    for level in range(1, levels + 1):
        heap = (1 << (levels - level)) - 1 + (row_index >> level)
        side = (row_index >> (level - 1)) & 1
        step_pick = node_pick[0, pl.ds(heap, 1), :] - side * SKEL
        picks = flags_dot(picks, picked(step_pick, SKEL))
        both = node_assign[0, pl.ds(heap, 1), :]
        step_assign = jnp.where(side == 0, both[:, :SKEL], both[:, SKEL:])
        assigns = flags_dot(picked(step_assign, SKEL), assigns)
    dim = points_ref.shape[0]
    root_points = jnp.zeros((dim, SKEL), F32)
    root_weights = jnp.zeros((values_ref.shape[0], SKEL), F32)
    for index in range(LPD):
        at = pl.ds(index * leaf, leaf)
        node = slice(index * SKEL, (index + 1) * SKEL)
        chosen = flags_dot(points_ref[:, at], picked(leaf_pick[index : index + 1, :], leaf))
        root_points += jnp.dot(chosen, picks[node], preferred_element_type=F32)
        spread = flags_dot(assigns[:, node], picked(leaf_assign[index : index + 1, :], SKEL))
        spread_ref[:, at] = spread
        root_weights += dot_back(values_ref[:, at], spread)
    share_ref[:dim, :] = root_points
    share_ref[dim:, :] = root_weights


def root_kernel(scale, where_ref, mask_ref, roots_ref, out_ref):
    count, rows, skel = roots_ref.shape
    cols = out_ref.shape[0]
    dim = rows - cols
    target = roots_ref[0, :dim, :].astype(BF16)
    target_norms = norm_rows(target, scale, False)
    total = jnp.zeros((cols, skel), F32)
    for index in range(1, count):
        source = roots_ref[index, :dim, :].astype(BF16)
        flag = mask_ref[0, where_ref[0] ^ index].astype(F32)
        kernel = jnp.exp2(
            jnp.dot(
                source_rows(source, scale),
                target_columns(target, target_norms),
                preferred_element_type=F32,
            )
        )
        weights = roots_ref[index, dim:, :] * flag
        total += jnp.dot(
            weights, kernel, preferred_element_type=F32, precision=lax.Precision.HIGHEST
        )
    out_ref[...] = total


def final_kernel(near_ref, root_ref, spread_ref, *refs):
    back_refs, out_ref = refs[:-1], refs[-1]
    total = near_ref[...]
    for part in split3(root_ref[...]):
        total += jnp.dot(part, spread_ref[...], preferred_element_type=F32)
    for back in back_refs:
        total += back[...].astype(F32)
    out_ref[...] = total


def shape(*dims, dtype=F32):
    return jax.ShapeDtypeStruct(dims, dtype)


def cost(flops, moved, exps=0):
    return pl.CostEstimate(flops=flops, bytes_accessed=moved, transcendentals=exps)


def on_device(
    points,
    vectors,
    leaf_pick,
    leaf_assign,
    device_pick,
    device_assign,
    node_pick,
    node_assign,
    far_mask,
    near_lower,
    near_upper,
):
    dim, device_cols = points.shape
    cols = vectors.shape[0]
    leaf = device_cols // LPD
    scale = 2.0 * KERNEL_RATE / dim * LOG2E
    width = 3 * dim + ROWS_AUG
    gx_count, reach = lax.axis_size("gx"), lax.axis_size("gy")
    levels = reach.bit_length() - 1
    slots = near_lower.shape[2]
    group = next(size for size in (4, 3, 2, 1) if slots % size == 0)
    where = jnp.stack([lax.axis_index("gx"), lax.axis_index("gy")]).astype(jnp.int32)
    tile_flops = 2 * leaf * leaf * (256 + 2 * 256)

    packed = jnp.concatenate([points, vectors], 0)
    others = {o: passed_along(packed, ("gx", "gy"), -o) for o in range(1, reach + 1)}

    share, spread = pl.pallas_call(
        functools.partial(rise_kernel, levels, leaf),
        out_shape=(shape(dim + cols, SKEL), shape(SKEL, device_cols, dtype=BF16)),
        in_specs=[SMEM] + [VMEM] * 8,
        out_specs=(VMEM, VMEM),
        cost_estimate=cost(2**28, 2**20),
        name="rise",
    )(where, points, vectors, leaf_pick, leaf_assign, device_pick, device_assign, node_pick, node_assign)
    for bit in range(levels):
        share = share + swapped(share, "gy", 1 << bit)
    roots = share[None]
    for bit in range(gx_count.bit_length() - 1):
        roots = jnp.concatenate([roots, swapped(roots, "gx", 1 << bit)], 0)

    rows, near = pl.pallas_call(
        functools.partial(self_kernel, scale, leaf),
        out_shape=(shape(device_cols, width, dtype=BF16), shape(cols, device_cols)),
        in_specs=[VMEM, VMEM],
        out_specs=(VMEM, VMEM),
        scratch_shapes=[
            pltpu.VMEM((ROWS_AUG, device_cols), BF16),
            pltpu.VMEM((LPD * (LPD + 1) // 2, leaf, leaf), BF16),
        ],
        cost_estimate=cost(10 * tile_flops, 2**21, 10 * leaf * leaf),
        name="own",
    )(points, vectors)
    backs = []
    for offset in range(reach, 0, -1):
        near, upper = pl.pallas_call(
            functools.partial(pair_kernel, scale, leaf, offset - 1, group),
            out_shape=(shape(cols, device_cols), shape(cols, device_cols, dtype=BF16)),
            in_specs=[SMEM, SMEM] + [VMEM] * 4,
            out_specs=(VMEM, VMEM),
            scratch_shapes=[
                pltpu.VMEM((ROWS_AUG, device_cols), BF16),
                pltpu.VMEM((cols, device_cols), F32),
                pltpu.VMEM((group, leaf, leaf), BF16),
            ],
            cost_estimate=cost(slots * tile_flops, 2**21, slots * leaf * leaf),
            name=f"near{offset}",
        )(near_lower, near_upper, rows, vectors, others[offset], near)
        backs.append(passed_along(upper, ("gx", "gy"), offset))
    root = pl.pallas_call(
        functools.partial(root_kernel, scale),
        out_shape=shape(cols, SKEL),
        in_specs=[SMEM, SMEM, VMEM],
        out_specs=VMEM,
        cost_estimate=cost(2**28, 2**20),
        name="roots",
    )(where, far_mask, roots)
    return pl.pallas_call(
        final_kernel,
        out_shape=shape(cols, device_cols),
        in_specs=[VMEM] * (3 + reach),
        out_specs=VMEM,
        cost_estimate=cost(2**26, 2**20),
        name="sum",
    )(near, root, spread, *backs)


def solution(mesh):
    placed = (
        P(None, ("gx", "gy")),
        P(None, ("gx", "gy")),
        P(("gx", "gy"), None),
        P(("gx", "gy"), None),
        P(("gx", "gy"), None),
        P(("gx", "gy"), None),
        P("gx", None, None),
        P("gx", None, None),
        P("gx", None),
        P(("gx", "gy"), None, None),
        P(("gx", "gy"), None, None),
    )
    return jax.shard_map(
        on_device, mesh=mesh, in_specs=placed, out_specs=P(None, ("gx", "gy")), check_vma=False
    )
```

time: 235 us -> 99.4 us (0.42)
  the two profiles are of different devices: /device:TPU:5 before, /device:TPU:1 now
where the time goes in v1:
time: 99.4 us; the launch traced here: 98.9 us
  Pallas kernels  42.6 us (43%)
  starting transfers between devices  33.5 us (34%)
  waiting for transfers between devices  14.7 us (15%)
  local copies, waits for them, and re-layouts  5.64 us (6%)
  other arithmetic  2.26 us (2%)
    pallas_call x4, Pallas kernels, on_device(): pl.pallas_call(functools.partial(pair_kernel, scale, leaf, offset - 1, gr...  29.2 us
    ppermute x8, starting transfers between devices, passed_along(): lax.ppermute(value, axis, [(source, source + steps) for source in range(f...  22.9 us
    ppermute x8, waiting for transfers between devices, passed_along(): lax.ppermute(value, axis, [(source, source + steps) for source in range(f...  11.5 us
    ppermute x5, starting transfers between devices, swapped(): return lax.ppermute(value, axis, pairs)  10.6 us
    unnamed x27, local copies, waits for them, and re-layouts  5.63 us
    pallas_call x1, Pallas kernels, on_device(): pl.pallas_call(functools.partial(self_kernel, scale, leaf), out_shape=(sh...  5.19 us
    ppermute x5, waiting for transfers between devices, swapped(): return lax.ppermute(value, axis, pairs)  3.14 us
    pallas_call x1, Pallas kernels, on_device(): pl.pallas_call(functools.partial(rise_kernel, levels, leaf), out_shape=(s...  3 us
  transfers between devices with their start and end apart: 13, of which 4 were waited for; matrix products, arithmetic and copies ran while one was open for 1% of the time, Pallas kernels for 38%

profile of v1, /device:TPU:1, one launch (start us, length us, event | category | flops | bytes accessed | tf_op | source)
XLA Modules:
  0.0 98.9 jit_solution(2961134380189015508)
XLA Ops:
  2.5 3.0 %rise.1 = (f32[96,128]{1,0:T(8,128)}, bf16[128,2048]{1,0:T(8,128)(2,1)}) custom-call(s32[2]{0:T(128)} %pad_add_fusion.where_ref, bf16[64,2048]{1,0:T(8,128)(2,1)} %points_ref.3, bf16[32,2048]{1,0:T(8,128)(2,1)} %values_ref.11, s32[4,128]{1,0:T(4,128)} %leaf_pick.1, s32[4,512]{1,0:T(4,128)} %leaf_assign.1, s32[1,128]{1,0:T(1,128)} %device_pick.1, ...), custom_call_target="tpu_custom_call" | custom-call | flops 268435456 | bytes 1048576 | tf_op jit(solution)/shard_map/rise/pallas_call | solution.py:271
  5.5 2.0 %collective-permute-start.4 = (f32[96,128]{1,0:T(8,128)}, f32[96,128]{1,0:T(8,128)S(1)}, u32[]{:S(2)}, u32[]{:S(2)}) collective-permute-start(f32[96,128]{1,0:T(8,128)} %get-tuple-element.23), channel_id=1, source_target_pairs={{0,1},{1,0},{2,3},{3,2},{4,5},{5,4},{6,7},{7,6},{8,9},{9,8},{10,11... | collective-permute-start | bytes 147464 | tf_op jit(solution)/shard_map/ppermute | solution.py:29
  7.5 1.7 %collective-permute-done.4 = f32[96,128]{1,0:T(8,128)S(1)} collective-permute-done((f32[96,128]{1,0:T(8,128)}, f32[96,128]{1,0:T(8,128)S(1)}, u32[]{:S(2)}, u32[]{:S(2)}) %collective-permute-start.4) | collective-permute-done | bytes 49184 | tf_op jit(solution)/shard_map/ppermute | solution.py:29
  10.0 1.5 %collective-permute-start.5 = (f32[96,128]{1,0:T(8,128)S(1)}, f32[96,128]{1,0:T(8,128)S(1)}, u32[]{:S(2)}, u32[]{:S(2)}) collective-permute-start(f32[96,128]{1,0:T(8,128)S(1)} %add.6), channel_id=1, source_target_pairs={{0,2},{1,3},{2,0},{3,1},{4,6},{5,7},{6,4},{7,5},{8,10},{9,11},{10,... | collective-permute-start | bytes 147464 | tf_op jit(solution)/shard_map/ppermute | solution.py:29
  11.6 1.4 %collective-permute-done.5 = f32[96,128]{1,0:T(8,128)S(1)} collective-permute-done((f32[96,128]{1,0:T(8,128)S(1)}, f32[96,128]{1,0:T(8,128)S(1)}, u32[]{:S(2)}, u32[]{:S(2)}) %collective-permute-start.5) | collective-permute-done | bytes 49184 | tf_op jit(solution)/shard_map/ppermute | solution.py:29
  13.0 2.8 %collective-permute-start.6 = (f32[1,96,128]{2,1,0:T(8,128)S(1)}, f32[1,96,128]{2,1,0:T(8,128)S(1)}, u32[]{:S(2)}, u32[]{:S(2)}) collective-permute-start(f32[1,96,128]{2,1,0:T(8,128)S(1)} %add_bitcast_fusion), channel_id=1, source_target_pairs={{0,4},{4,0},{8,12},{12,8},{16,20},{20,16},{24,28},{28,24},{1,5},{5... | collective-permute-start | bytes 147464 | tf_op jit(solution)/shard_map/ppermute | solution.py:29
  15.8 4.5 %collective-permute-start = (bf16[96,2048]{1,0:T(8,128)(2,1)S(1)}, bf16[96,2048]{1,0:T(8,128)(2,1)S(1)}, u32[]{:S(2)}, u32[]{:S(2)}) collective-permute-start(bf16[96,2048]{1,0:T(8,128)(2,1)S(1)} %constant_dynamic-update-slice_fusion), channel_id=1, source_target_pairs={{1,0},{2,1},{3,2},{4,3},{5,4},{6,5},{7,6},{8,7},{9,8},{10,9},{11,1... | collective-permute-start | bytes 1179656 | tf_op jit(solution)/shard_map/ppermute | solution.py:24
  20.3 2.4 %collective-permute-start.1 = (bf16[96,2048]{1,0:T(8,128)(2,1)S(1)}, bf16[96,2048]{1,0:T(8,128)(2,1)S(1)}, u32[]{:S(2)}, u32[]{:S(2)}) collective-permute-start(bf16[96,2048]{1,0:T(8,128)(2,1)S(1)} %constant_dynamic-update-slice_fusion), channel_id=1, source_target_pairs={{2,0},{3,1},{4,2},{5,3},{6,4},{7,5},{8,6},{9,7},{10,8},{11,9},{12,... | collective-permute-start | bytes 1179656 | tf_op jit(solution)/shard_map/ppermute | solution.py:24
  22.7 1.9 %collective-permute-start.2 = (bf16[96,2048]{1,0:T(8,128)(2,1)S(1)}, bf16[96,2048]{1,0:T(8,128)(2,1)S(1)}, u32[]{:S(2)}, u32[]{:S(2)}) collective-permute-start(bf16[96,2048]{1,0:T(8,128)(2,1)S(1)} %constant_dynamic-update-slice_fusion), channel_id=1, source_target_pairs={{3,0},{4,1},{5,2},{6,3},{7,4},{8,5},{9,6},{10,7},{11,8},{12,9},{13... | collective-permute-start | bytes 1179656 | tf_op jit(solution)/shard_map/ppermute | solution.py:24
  24.6 1.9 %collective-permute-start.3 = (bf16[96,2048]{1,0:T(8,128)(2,1)S(1)}, bf16[96,2048]{1,0:T(8,128)(2,1)S(1)}, u32[]{:S(2)}, u32[]{:S(2)}) collective-permute-start(bf16[96,2048]{1,0:T(8,128)(2,1)S(1)} %constant_dynamic-update-slice_fusion), channel_id=1, source_target_pairs={{4,0},{5,1},{6,2},{7,3},{8,4},{9,5},{10,6},{11,7},{12,8},{13,9},{1... | collective-permute-start | bytes 1179656 | tf_op jit(solution)/shard_map/ppermute | solution.py:24
  26.6 1.9 %collective-permute-start.7 = (f32[2,96,128]{2,1,0:T(8,128)S(1)}, f32[2,96,128]{2,1,0:T(8,128)S(1)}, u32[]{:S(2)}, u32[]{:S(2)}) collective-permute-start(f32[2,96,128]{2,1,0:T(8,128)S(1)} %pad_maximum_fusion.2), channel_id=1, source_target_pairs={{0,8},{4,12},{8,0},{12,4},{16,24},{20,28},{24,16},{28,20},{1,9},{5... | collective-permute-start | bytes 294920 | tf_op jit(solution)/shard_map/ppermute | solution.py:29
  28.5 5.2 %own.1 = (bf16[2048,208]{1,0:T(8,128)(2,1)}, f32[32,2048]{1,0:T(8,128)}) custom-call(bf16[64,2048]{1,0:T(8,128)(2,1)} %points_ref.3, bf16[32,2048]{1,0:T(8,128)(2,1)} %values_ref.11), custom_call_target="tpu_custom_call" | custom-call | flops 4026531840 | bytes 2097152 | tf_op jit(solution)/shard_map/own/pallas_call | solution.py:285
  33.7 2.4 %collective-permute-start.8 = (f32[4,96,128]{2,1,0:T(8,128)S(1)}, f32[4,96,128]{2,1,0:T(8,128)S(1)}, u32[]{:S(2)}, u32[]{:S(2)}) collective-permute-start(f32[4,96,128]{2,1,0:T(8,128)S(1)} %pad_maximum_fusion.1), channel_id=1, source_target_pairs={{0,16},{4,20},{8,24},{12,28},{16,0},{20,4},{24,8},{28,12},{1,17},{... | collective-permute-start | bytes 589832 | tf_op jit(solution)/shard_map/ppermute | solution.py:29
  36.1 10.1 %collective-permute-done.3.other_ref = bf16[96,2048]{1,0:T(8,128)(2,1)S(1)} collective-permute-done((bf16[96,2048]{1,0:T(8,128)(2,1)S(1)}, bf16[96,2048]{1,0:T(8,128)(2,1)S(1)}, u32[]{:S(2)}, u32[]{:S(2)}) %collective-permute-start.3) | collective-permute-done | bytes 393248 | tf_op jit(solution)/shard_map/ppermute | solution.py:24
  47.0 7.3 %near4.1 = (f32[32,2048]{1,0:T(8,128)}, bf16[32,2048]{1,0:T(8,128)(2,1)}) custom-call(s32[1,4,12]{2,1,0:T(4,128)} %lower_ref.7, s32[1,4,12]{2,1,0:T(4,128)} %upper_ref.7, bf16[2048,208]{1,0:T(8,128)(2,1)} %get-tuple-element.17.rows_ref, bf16[32,2048]{1,0:T(8,128)(2,1)} %values_ref.11, bf16[96,2048]{1,0:T(8,128)(2,1)} %copy-done.11, ...), custom_call_target="tpu_custom_call" | custom-call | flops 4831838208 | bytes 2097152 | tf_op jit(solution)/shard_map/near4/pallas_call | solution.py:299
  54.4 5.0 %collective-permute-start.9 = (bf16[32,2048]{1,0:T(8,128)(2,1)}, bf16[32,2048]{1,0:T(8,128)(2,1)S(1)}, u32[]{:S(2)}, u32[]{:S(2)}) collective-permute-start(bf16[32,2048]{1,0:T(8,128)(2,1)} %get-tuple-element.25), channel_id=1, source_target_pairs={{0,4},{1,5},{2,6},{3,7},{4,8},{5,9},{6,10},{7,11},{8,12},{9,13},{1... | collective-permute-start | bytes 393224 | tf_op jit(solution)/shard_map/ppermute | solution.py:24
  60.2 7.3 %near3.1 = (f32[32,2048]{1,0:T(8,128)}, bf16[32,2048]{1,0:T(8,128)(2,1)}) custom-call(s32[1,4,12]{2,1,0:T(4,128)} %lower_ref.7, s32[1,4,12]{2,1,0:T(4,128)} %upper_ref.7, bf16[2048,208]{1,0:T(8,128)(2,1)} %get-tuple-element.17.rows_ref, bf16[32,2048]{1,0:T(8,128)(2,1)} %values_ref.11, bf16[96,2048]{1,0:T(8,128)(2,1)} %copy-done.10, ...), custom_call_target="tpu_custom_call" | custom-call | flops 4831838208 | bytes 2097152 | tf_op jit(solution)/shard_map/near3/pallas_call | solution.py:299
  67.5 1.9 %collective-permute-start.10 = (bf16[32,2048]{1,0:T(8,128)(2,1)}, bf16[32,2048]{1,0:T(8,128)(2,1)S(1)}, u32[]{:S(2)}, u32[]{:S(2)}) collective-permute-start(bf16[32,2048]{1,0:T(8,128)(2,1)} %get-tuple-element.26), channel_id=1, source_target_pairs={{0,3},{1,4},{2,5},{3,6},{4,7},{5,8},{6,9},{7,10},{8,11},{9,12},{10... | collective-permute-start | bytes 393224 | tf_op jit(solution)/shard_map/ppermute | solution.py:24
  70.2 7.3 %near2.1 = (f32[32,2048]{1,0:T(8,128)}, bf16[32,2048]{1,0:T(8,128)(2,1)}) custom-call(s32[1,4,12]{2,1,0:T(4,128)} %lower_ref.7, s32[1,4,12]{2,1,0:T(4,128)} %upper_ref.7, bf16[2048,208]{1,0:T(8,128)(2,1)} %get-tuple-element.17.rows_ref, bf16[32,2048]{1,0:T(8,128)(2,1)} %values_ref.11, bf16[96,2048]{1,0:T(8,128)(2,1)} %copy-done.9, ...), custom_call_target="tpu_custom_call" | custom-call | flops 4831838208 | bytes 2097152 | tf_op jit(solution)/shard_map/near2/pallas_call | solution.py:299
  77.5 2.9 %collective-permute-start.11 = (bf16[32,2048]{1,0:T(8,128)(2,1)}, bf16[32,2048]{1,0:T(8,128)(2,1)S(1)}, u32[]{:S(2)}, u32[]{:S(2)}) collective-permute-start(bf16[32,2048]{1,0:T(8,128)(2,1)} %get-tuple-element.27), channel_id=1, source_target_pairs={{0,2},{1,3},{2,4},{3,5},{4,6},{5,7},{6,8},{7,9},{8,10},{9,11},{10,... | collective-permute-start | bytes 393224 | tf_op jit(solution)/shard_map/ppermute | solution.py:24
  81.2 7.3 %near1.1 = (f32[32,2048]{1,0:T(8,128)}, bf16[32,2048]{1,0:T(8,128)(2,1)}) custom-call(s32[1,4,12]{2,1,0:T(4,128)} %lower_ref.7, s32[1,4,12]{2,1,0:T(4,128)} %upper_ref.7, bf16[2048,208]{1,0:T(8,128)(2,1)} %get-tuple-element.17.rows_ref, bf16[32,2048]{1,0:T(8,128)(2,1)} %values_ref.11, bf16[96,2048]{1,0:T(8,128)(2,1)} %copy-done.8, ...), custom_call_target="tpu_custom_call" | custom-call | flops 4831838208 | bytes 2097152 | tf_op jit(solution)/shard_map/near1/pallas_call | solution.py:299
  88.5 2.3 %collective-permute-start.12 = (bf16[32,2048]{1,0:T(8,128)(2,1)}, bf16[32,2048]{1,0:T(8,128)(2,1)S(1)}, u32[]{:S(2)}, u32[]{:S(2)}) collective-permute-start(bf16[32,2048]{1,0:T(8,128)(2,1)} %get-tuple-element.28), channel_id=1, source_target_pairs={{0,1},{1,2},{2,3},{3,4},{4,5},{5,6},{6,7},{7,8},{8,9},{9,10},{10,1... | collective-permute-start | bytes 393224 | tf_op jit(solution)/shard_map/ppermute | solution.py:24
  91.6 2.8 %roots.1.root_ref = f32[32,128]{1,0:T(8,128)} custom-call(s32[2]{0:T(128)} %pad_add_fusion.where_ref, s32[1,8]{1,0:T(1,128)} %mask_ref.1, f32[8,96,128]{2,1,0:T(8,128)} %pad_maximum_fusion.roots_ref), custom_call_target="tpu_custom_call" | custom-call | flops 268435456 | bytes 1048576 | tf_op jit(solution)/shard_map/roots/pallas_call | solution.py:313
  96.5 2.4 %sum.1 = f32[32,2048]{1,0:T(8,128)} custom-call(f32[32,2048]{1,0:T(8,128)} %get-tuple-element.22.near_ref, f32[32,128]{1,0:T(8,128)} %roots.1.root_ref, bf16[128,2048]{1,0:T(8,128)(2,1)} %get-tuple-element.24.spread_ref, bf16[32,2048]{1,0:T(8,128)(2,1)} %copy-done.1, bf16[32,2048]{1,0:T(8,128)(2,1)} %copy-done.2, bf16[32,2048]{1,0:T(8,128)(2,1)} %copy-done.3, ...), custom_call_target="tpu_custom_call" | custom-call | flops 67108864 | bytes 1048576 | tf_op jit(solution)/shard_map/sum/pallas_call | solution.py:321
  (44 shorter events, 9.3 us)
Async XLA Ops:
  0.0 0.7 copy-start.7
  0.0 1.3 %copy-start.6 = (s32[1,3,256]{2,0,1:T(1,128)S(1)}, s32[1,3,256]{2,0,1:T(1,128)}, u32[]{:S(2)}) copy-start(s32[1,3,256]{2,0,1:T(1,128)} %param.18) | copy-start | bytes 9220
  2.5 9.0 %copy-start = (bf16[64,2048]{1,0:T(8,128)(2,1)S(1)}, bf16[64,2048]{1,0:T(8,128)(2,1)}, u32[]{:S(2)}) copy-start(bf16[64,2048]{1,0:T(8,128)(2,1)} %points_ref.3) | copy-start | bytes 786436
  5.5 3.7 %collective-permute-start.4 = (f32[96,128]{1,0:T(8,128)}, f32[96,128]{1,0:T(8,128)S(1)}, u32[]{:S(2)}, u32[]{:S(2)}) collective-permute-start(f32[96,128]{1,0:T(8,128)} %get-tuple-element.23), channel_id=1, source_target_pairs={{0,1},{1,0},{2,3},{3,2},{4,5},{5,4},{6,7},{7,6},{8,9},{9,8},{10,11... | collective-permute-start | bytes 147464 | tf_op jit(solution)/shard_map/ppermute | solution.py:29
  10.0 3.0 %collective-permute-start.5 = (f32[96,128]{1,0:T(8,128)S(1)}, f32[96,128]{1,0:T(8,128)S(1)}, u32[]{:S(2)}, u32[]{:S(2)}) collective-permute-start(f32[96,128]{1,0:T(8,128)S(1)} %add.6), channel_id=1, source_target_pairs={{0,2},{1,3},{2,0},{3,1},{4,6},{5,7},{6,4},{7,5},{8,10},{9,11},{10,... | collective-permute-start | bytes 147464 | tf_op jit(solution)/shard_map/ppermute | solution.py:29
  11.5 4.2 %copy-start.5 = (bf16[32,2048]{1,0:T(8,128)(2,1)S(1)}, bf16[32,2048]{1,0:T(8,128)(2,1)}, u32[]{:S(2)}) copy-start(bf16[32,2048]{1,0:T(8,128)(2,1)} %values_ref.11) | copy-start | bytes 393220
  13.0 13.5 %collective-permute-start.6 = (f32[1,96,128]{2,1,0:T(8,128)S(1)}, f32[1,96,128]{2,1,0:T(8,128)S(1)}, u32[]{:S(2)}, u32[]{:S(2)}) collective-permute-start(f32[1,96,128]{2,1,0:T(8,128)S(1)} %add_bitcast_fusion), channel_id=1, source_target_pairs={{0,4},{4,0},{8,12},{12,8},{16,20},{20,16},{24,28},{28,24},{1,5},{5... | collective-permute-start | bytes 147464 | tf_op jit(solution)/shard_map/ppermute | solution.py:29
  15.8 64.6 %collective-permute-start = (bf16[96,2048]{1,0:T(8,128)(2,1)S(1)}, bf16[96,2048]{1,0:T(8,128)(2,1)S(1)}, u32[]{:S(2)}, u32[]{:S(2)}) collective-permute-start(bf16[96,2048]{1,0:T(8,128)(2,1)S(1)} %constant_dynamic-update-slice_fusion), channel_id=1, source_target_pairs={{1,0},{2,1},{3,2},{4,3},{5,4},{6,5},{7,6},{8,7},{9,8},{10,9},{11,1... | collective-permute-start | bytes 1179656 | tf_op jit(solution)/shard_map/ppermute | solution.py:24
  20.3 49.1 %collective-permute-start.1 = (bf16[96,2048]{1,0:T(8,128)(2,1)S(1)}, bf16[96,2048]{1,0:T(8,128)(2,1)S(1)}, u32[]{:S(2)}, u32[]{:S(2)}) collective-permute-start(bf16[96,2048]{1,0:T(8,128)(2,1)S(1)} %constant_dynamic-update-slice_fusion), channel_id=1, source_target_pairs={{2,0},{3,1},{4,2},{5,3},{6,4},{7,5},{8,6},{9,7},{10,8},{11,9},{12,... | collective-permute-start | bytes 1179656 | tf_op jit(solution)/shard_map/ppermute | solution.py:24
  22.7 36.7 %collective-permute-start.2 = (bf16[96,2048]{1,0:T(8,128)(2,1)S(1)}, bf16[96,2048]{1,0:T(8,128)(2,1)S(1)}, u32[]{:S(2)}, u32[]{:S(2)}) collective-permute-start(bf16[96,2048]{1,0:T(8,128)(2,1)S(1)} %constant_dynamic-update-slice_fusion), channel_id=1, source_target_pairs={{3,0},{4,1},{5,2},{6,3},{7,4},{8,5},{9,6},{10,7},{11,8},{12,9},{13... | collective-permute-start | bytes 1179656 | tf_op jit(solution)/shard_map/ppermute | solution.py:24
  24.6 21.6 %collective-permute-start.3 = (bf16[96,2048]{1,0:T(8,128)(2,1)S(1)}, bf16[96,2048]{1,0:T(8,128)(2,1)S(1)}, u32[]{:S(2)}, u32[]{:S(2)}) collective-permute-start(bf16[96,2048]{1,0:T(8,128)(2,1)S(1)} %constant_dynamic-update-slice_fusion), channel_id=1, source_target_pairs={{4,0},{5,1},{6,2},{7,3},{8,4},{9,5},{10,6},{11,7},{12,8},{13,9},{1... | collective-permute-start | bytes 1179656 | tf_op jit(solution)/shard_map/ppermute | solution.py:24
  26.6 7.1 %collective-permute-start.7 = (f32[2,96,128]{2,1,0:T(8,128)S(1)}, f32[2,96,128]{2,1,0:T(8,128)S(1)}, u32[]{:S(2)}, u32[]{:S(2)}) collective-permute-start(f32[2,96,128]{2,1,0:T(8,128)S(1)} %pad_maximum_fusion.2), channel_id=1, source_target_pairs={{0,8},{4,12},{8,0},{12,4},{16,24},{20,28},{24,16},{28,20},{1,9},{5... | collective-permute-start | bytes 294920 | tf_op jit(solution)/shard_map/ppermute | solution.py:29
  33.7 57.1 %collective-permute-start.8 = (f32[4,96,128]{2,1,0:T(8,128)S(1)}, f32[4,96,128]{2,1,0:T(8,128)S(1)}, u32[]{:S(2)}, u32[]{:S(2)}) collective-permute-start(f32[4,96,128]{2,1,0:T(8,128)S(1)} %pad_maximum_fusion.1), channel_id=1, source_target_pairs={{0,16},{4,20},{8,24},{12,28},{16,0},{20,4},{24,8},{28,12},{1,17},{... | collective-permute-start | bytes 589832 | tf_op jit(solution)/shard_map/ppermute | solution.py:29
  46.3 0.8 copy-start.11
  54.4 40.1 %collective-permute-start.9 = (bf16[32,2048]{1,0:T(8,128)(2,1)}, bf16[32,2048]{1,0:T(8,128)(2,1)S(1)}, u32[]{:S(2)}, u32[]{:S(2)}) collective-permute-start(bf16[32,2048]{1,0:T(8,128)(2,1)} %get-tuple-element.25), channel_id=1, source_target_pairs={{0,4},{1,5},{2,6},{3,7},{4,8},{5,9},{6,10},{7,11},{8,12},{9,13},{1... | collective-permute-start | bytes 393224 | tf_op jit(solution)/shard_map/ppermute | solution.py:24
  59.4 0.8 copy-start.10
  67.5 26.9 %collective-permute-start.10 = (bf16[32,2048]{1,0:T(8,128)(2,1)}, bf16[32,2048]{1,0:T(8,128)(2,1)S(1)}, u32[]{:S(2)}, u32[]{:S(2)}) collective-permute-start(bf16[32,2048]{1,0:T(8,128)(2,1)} %get-tuple-element.26), channel_id=1, source_target_pairs={{0,3},{1,4},{2,5},{3,6},{4,7},{5,8},{6,9},{7,10},{8,11},{9,12},{10... | collective-permute-start | bytes 393224 | tf_op jit(solution)/shard_map/ppermute | solution.py:24
  69.4 0.8 copy-start.9
  77.5 17.0 %collective-permute-start.11 = (bf16[32,2048]{1,0:T(8,128)(2,1)}, bf16[32,2048]{1,0:T(8,128)(2,1)S(1)}, u32[]{:S(2)}, u32[]{:S(2)}) collective-permute-start(bf16[32,2048]{1,0:T(8,128)(2,1)} %get-tuple-element.27), channel_id=1, source_target_pairs={{0,2},{1,3},{2,4},{3,5},{4,6},{5,7},{6,8},{7,9},{8,10},{9,11},{10,... | collective-permute-start | bytes 393224 | tf_op jit(solution)/shard_map/ppermute | solution.py:24
  80.4 0.8 copy-start.8
  88.5 7.4 %collective-permute-start.12 = (bf16[32,2048]{1,0:T(8,128)(2,1)}, bf16[32,2048]{1,0:T(8,128)(2,1)S(1)}, u32[]{:S(2)}, u32[]{:S(2)}) collective-permute-start(bf16[32,2048]{1,0:T(8,128)(2,1)} %get-tuple-element.28), channel_id=1, source_target_pairs={{0,1},{1,2},{2,3},{3,4},{4,5},{5,6},{6,7},{7,8},{8,9},{9,10},{10,1... | collective-permute-start | bytes 393224 | tf_op jit(solution)/shard_map/ppermute | solution.py:24
  94.4 1.4 %copy-start.1 = (bf16[32,2048]{1,0:T(8,128)(2,1)}, bf16[32,2048]{1,0:T(8,128)(2,1)S(1)}, u32[]{:S(2)}) copy-start(bf16[32,2048]{1,0:T(8,128)(2,1)S(1)} %collective-permute-done.9.refs_0_) | copy-start | bytes 393220
  94.4 1.4 %copy-start.2 = (bf16[32,2048]{1,0:T(8,128)(2,1)}, bf16[32,2048]{1,0:T(8,128)(2,1)S(1)}, u32[]{:S(2)}) copy-start(bf16[32,2048]{1,0:T(8,128)(2,1)S(1)} %collective-permute-done.10.refs_1_) | copy-start | bytes 393220
  94.5 1.4 %copy-start.3 = (bf16[32,2048]{1,0:T(8,128)(2,1)}, bf16[32,2048]{1,0:T(8,128)(2,1)S(1)}, u32[]{:S(2)}) copy-start(bf16[32,2048]{1,0:T(8,128)(2,1)S(1)} %collective-permute-done.11.refs_2_) | copy-start | bytes 393220
  (1 other events, 0.7 us)

commit v2 on v1

--- a/solution.py
+++ b/solution.py
@@ -94,8 +94,10 @@
 def pair_kernel(
     scale,
     leaf,
-    offset,
+    reach,
+    partner,
     group,
+    where_ref,
     lower_ref,
     upper_ref,
     rows_ref,
@@ -109,7 +111,8 @@
     tiles_ref,
 ):
     dim = other_ref.shape[0] - values_ref.shape[0]
-    near_ref[...] = near_in[...]
+    row_index = where_ref[1]
+    offset = lax.rem((row_index ^ partner) - row_index + reach - 1, reach)
     upper_sum[...] = jnp.zeros_like(upper_sum)
     norms_ref[...] = norm_rows(other_ref[:dim, :], scale, False)
 
@@ -160,28 +163,22 @@
 def rise_kernel(
     levels,
     leaf,
-    where_ref,
     points_ref,
     values_ref,
     leaf_pick,
     leaf_assign,
     device_pick,
     device_assign,
-    node_pick,
-    node_assign,
+    tables_ref,
     share_ref,
     spread_ref,
 ):
-    row_index = where_ref[1]
     picks = picked(device_pick[...], LPD * SKEL)
     assigns = picked(device_assign[...], SKEL)
-    for level in range(1, levels + 1):
-        heap = (1 << (levels - level)) - 1 + (row_index >> level)
-        side = (row_index >> (level - 1)) & 1
-        step_pick = node_pick[0, pl.ds(heap, 1), :] - side * SKEL
+    for level in range(levels):
+        step_pick = tables_ref[2 * level : 2 * level + 1, :]
+        step_assign = tables_ref[2 * level + 1 : 2 * level + 2, :]
         picks = flags_dot(picks, picked(step_pick, SKEL))
-        both = node_assign[0, pl.ds(heap, 1), :]
-        step_assign = jnp.where(side == 0, both[:, :SKEL], both[:, SKEL:])
         assigns = flags_dot(picked(step_assign, SKEL), assigns)
     dim = points_ref.shape[0]
     root_points = jnp.zeros((dim, SKEL), F32)
@@ -199,41 +196,44 @@
 
 
 def root_kernel(scale, where_ref, mask_ref, roots_ref, out_ref):
-    count, rows, skel = roots_ref.shape
-    cols = out_ref.shape[0]
-    dim = rows - cols
-    target = roots_ref[0, :dim, :].astype(BF16)
-    target_norms = norm_rows(target, scale, False)
-    total = jnp.zeros((cols, skel), F32)
-    for index in range(1, count):
-        source = roots_ref[index, :dim, :].astype(BF16)
-        flag = mask_ref[0, where_ref[0] ^ index].astype(F32)
-        kernel = jnp.exp2(
-            jnp.dot(
-                source_rows(source, scale),
-                target_columns(target, target_norms),
-                preferred_element_type=F32,
-            )
-        )
-        weights = roots_ref[index, dim:, :] * flag
-        total += jnp.dot(
-            weights, kernel, preferred_element_type=F32, precision=lax.Precision.HIGHEST
-        )
-    out_ref[...] = total
-
-
-def final_kernel(near_ref, root_ref, spread_ref, *refs):
-    back_refs, out_ref = refs[:-1], refs[-1]
+    count, cols = roots_ref.shape[0], out_ref.shape[0]
+    dim = roots_ref.shape[1] - cols
+    target = source_rows(roots_ref[0, :dim, :].astype(BF16), scale)
+    flags = [mask_ref[0, where_ref[0] ^ index].astype(F32) for index in range(1, count)]
+    weights = [roots_ref[index, dim:, :] * flag for index, flag in enumerate(flags, 1)]
+    sources = [roots_ref[index, :dim, :].astype(BF16) for index in range(1, count)]
+    source = jnp.concatenate(sources, 1)
+    product = jnp.dot(
+        target,
+        target_columns(source, norm_rows(source, scale, False)),
+        preferred_element_type=F32,
+    )
+    out_ref[...] = lax.dot_general(
+        jnp.concatenate(weights, 1),
+        jnp.exp2(product),
+        (((1,), (1,)), ((), ())),
+        preferred_element_type=F32,
+        precision=lax.Precision.HIGHEST,
+    )
+
+
+def fall_kernel(near_ref, root_ref, spread_ref, out_ref):
     total = near_ref[...]
     for part in split3(root_ref[...]):
         total += jnp.dot(part, spread_ref[...], preferred_element_type=F32)
-    for back in back_refs:
-        total += back[...].astype(F32)
     out_ref[...] = total
 
 
 def shape(*dims, dtype=F32):
     return jax.ShapeDtypeStruct(dims, dtype)
+
+
+def kept(*dims, dtype=F32):
+    return pltpu.VMEM(dims, dtype)
+
+
+def held(value):
+    return pltpu.with_memory_space_constraint(value, pltpu.VMEM)
 
 
 def cost(flops, moved, exps=0):
@@ -262,20 +262,31 @@
     levels = reach.bit_length() - 1
     slots = near_lower.shape[2]
     group = next(size for size in (4, 3, 2, 1) if slots % size == 0)
-    where = jnp.stack([lax.axis_index("gx"), lax.axis_index("gy")]).astype(jnp.int32)
+    row_index = lax.axis_index("gy")
+    where = jnp.stack([lax.axis_index("gx"), row_index]).astype(jnp.int32)
     tile_flops = 2 * leaf * leaf * (256 + 2 * 256)
 
+    def side_of(level):
+        return (row_index >> (level - 1)) & 1
+
     packed = jnp.concatenate([points, vectors], 0)
-    others = {o: passed_along(packed, ("gx", "gy"), -o) for o in range(1, reach + 1)}
-
+    ahead = passed_along(packed, "gx", -1)
+
+    tables = []
+    for level in range(1, levels + 1):
+        heap = (reach >> level) - 1 + (row_index >> level)
+        tables.append(lax.dynamic_slice(node_pick[0], (heap, 0), (1, SKEL)) - side_of(level) * SKEL)
+        tables.append(
+            lax.dynamic_slice(node_assign[0], (heap, side_of(level) * SKEL), (1, SKEL))
+        )
     share, spread = pl.pallas_call(
         functools.partial(rise_kernel, levels, leaf),
-        out_shape=(shape(dim + cols, SKEL), shape(SKEL, device_cols, dtype=BF16)),
-        in_specs=[SMEM] + [VMEM] * 8,
+        out_shape=(shape(dim + cols, SKEL), kept(SKEL, device_cols, dtype=BF16)),
+        in_specs=[VMEM] * 7,
         out_specs=(VMEM, VMEM),
         cost_estimate=cost(2**28, 2**20),
         name="rise",
-    )(where, points, vectors, leaf_pick, leaf_assign, device_pick, device_assign, node_pick, node_assign)
+    )(points, vectors, leaf_pick, leaf_assign, device_pick, device_assign, jnp.concatenate(tables, 0))
     for bit in range(levels):
         share = share + swapped(share, "gy", 1 << bit)
     roots = share[None]
@@ -284,7 +295,7 @@
 
     rows, near = pl.pallas_call(
         functools.partial(self_kernel, scale, leaf),
-        out_shape=(shape(device_cols, width, dtype=BF16), shape(cols, device_cols)),
+        out_shape=(kept(device_cols, width, dtype=BF16), kept(cols, device_cols)),
         in_specs=[VMEM, VMEM],
         out_specs=(VMEM, VMEM),
         scratch_shapes=[
@@ -294,22 +305,38 @@
         cost_estimate=cost(10 * tile_flops, 2**21, 10 * leaf * leaf),
         name="own",
     )(points, vectors)
-    backs = []
-    for offset in range(reach, 0, -1):
-        near, upper = pl.pallas_call(
-            functools.partial(pair_kernel, scale, leaf, offset - 1, group),
-            out_shape=(shape(cols, device_cols), shape(cols, device_cols, dtype=BF16)),
-            in_specs=[SMEM, SMEM] + [VMEM] * 4,
+
+    def meet(partner, other, near):
+        return pl.pallas_call(
+            functools.partial(pair_kernel, scale, leaf, reach, partner, group),
+            out_shape=(kept(cols, device_cols), shape(cols, device_cols, dtype=BF16)),
+            in_specs=[SMEM] * 3 + [VMEM] * 4,
             out_specs=(VMEM, VMEM),
             scratch_shapes=[
                 pltpu.VMEM((ROWS_AUG, device_cols), BF16),
                 pltpu.VMEM((cols, device_cols), F32),
                 pltpu.VMEM((group, leaf, leaf), BF16),
             ],
+            input_output_aliases={6: 0},
             cost_estimate=cost(slots * tile_flops, 2**21, slots * leaf * leaf),
-            name=f"near{offset}",
-        )(near_lower, near_upper, rows, vectors, others[offset], near)
-        backs.append(passed_along(upper, ("gx", "gy"), offset))
+            name=f"near{partner}",
+        )(where, near_lower, near_upper, held(rows), vectors, held(other), held(near))
+
+    others = {}
+    for bit in range(levels):
+        payload = jnp.where(side_of(bit + 1) == 1, packed, ahead)
+        for partner in range(1 << bit, 2 << bit):
+            others[partner] = swapped(payload, "gy", partner)
+    mine, onward = [], []
+    for partner in range(1, reach):
+        near, upper = meet(partner, others[partner], near)
+        back = swapped(upper, "gy", partner).astype(F32)
+        upper_side = side_of(partner.bit_length()) == 1
+        mine.append(jnp.where(upper_side, back, 0.0))
+        onward.append(jnp.where(upper_side, 0.0, back))
+    near, upper = meet(0, ahead, near)
+    forward = functools.reduce(jnp.add, onward, upper.astype(F32)).astype(BF16)
+    landed = passed_along(forward, "gx", 1)
     root = pl.pallas_call(
         functools.partial(root_kernel, scale),
         out_shape=shape(cols, SKEL),
@@ -318,14 +345,15 @@
         cost_estimate=cost(2**28, 2**20),
         name="roots",
     )(where, far_mask, roots)
-    return pl.pallas_call(
-        final_kernel,
+    local = pl.pallas_call(
+        fall_kernel,
         out_shape=shape(cols, device_cols),
-        in_specs=[VMEM] * (3 + reach),
+        in_specs=[VMEM] * 3,
         out_specs=VMEM,
         cost_estimate=cost(2**26, 2**20),
-        name="sum",
-    )(near, root, spread, *backs)
+        name="fall",
+    )(held(near), root, held(spread))
+    return functools.reduce(jnp.add, mine, local) + landed.astype(F32)
 
 
 def solution(mesh):

time: 99.4 us -> 87.5 us (0.88)
  the two profiles are of different devices: /device:TPU:1 before, /device:TPU:5 now
where the time goes in v2:
time: 87.5 us; the launch traced here: 86.6 us
  Pallas kernels  38.3 us (44%)
  starting transfers between devices  20.4 us (23%)
  waiting for transfers between devices  17.9 us (20%)
  other arithmetic  7.49 us (9%)
  local copies, waits for them, and re-layouts  2.37 us (3%)
    pallas_call x4, Pallas kernels, meet(): pl.pallas_call(functools.partial(pair_kernel, scale, leaf, reach, partner...  26.8 us
    ppermute x11, waiting for transfers between devices, swapped(): return lax.ppermute(value, axis, pairs)  17.9 us
    ppermute x11, starting transfers between devices, swapped(): return lax.ppermute(value, axis, pairs)  12.2 us
    ppermute x2, starting transfers between devices, passed_along(): lax.ppermute(value, axis, [(source, source + steps) for source in range(f...  8.18 us
    pallas_call x1, Pallas kernels, on_device(): pl.pallas_call(functools.partial(self_kernel, scale, leaf), out_shape=(ke...  4.46 us
    pallas_call x1, Pallas kernels, on_device(): pl.pallas_call(functools.partial(rise_kernel, levels, leaf), out_shape=(s...  2.88 us
    pallas_call x1, Pallas kernels, on_device(): pl.pallas_call(functools.partial(root_kernel, scale), out_shape=shape(col...  2.43 us
    pallas_call x1, Pallas kernels, on_device(): pl.pallas_call(fall_kernel, out_shape=shape(cols, device_cols), in_specs=...  1.76 us
  transfers between devices with their start and end apart: 13, of which 4 were waited for; matrix products, arithmetic and copies ran while one was open for 7% of the time, Pallas kernels for 44%

profile of v2, /device:TPU:5, one launch (start us, length us, event | category | flops | bytes accessed | tf_op | source)
XLA Modules:
  0.0 86.6 jit_solution(1464289475863091554)
XLA Ops:
  0.0 1.0 %constant_dynamic-update-slice_fusion.1 = bf16[96,2048]{1,0:T(8,128)(2,1)S(1)} fusion(bf16[64,2048]{1,0:T(8,128)(2,1)} %points_ref.3), kind=kLoop, calls=%fused_computation.21 | loop fusion | bytes 524288
  1.0 2.6 %collective-permute-start = (bf16[96,2048]{1,0:T(8,128)(2,1)S(1)}, bf16[96,2048]{1,0:T(8,128)(2,1)S(1)}, u32[]{:S(2)}, u32[]{:S(2)}) collective-permute-start(bf16[96,2048]{1,0:T(8,128)(2,1)S(1)} %constant_dynamic-update-slice_fusion), channel_id=1, source_target_pairs={{4,0},{8,4},{12,8},{16,12},{20,16},{24,20},{28,24},{5,1},{9,5},{13... | collective-permute-start | bytes 1179656 | tf_op jit(solution)/shard_map/ppermute | solution.py:24
  5.6 2.9 %rise.1 = (f32[96,128]{1,0:T(8,128)}, bf16[128,2048]{1,0:T(8,128)(2,1)S(1)}) custom-call(bf16[64,2048]{1,0:T(8,128)(2,1)} %points_ref.3, bf16[32,2048]{1,0:T(8,128)(2,1)} %values_ref.11, s32[4,128]{1,0:T(4,128)} %leaf_pick.1, s32[4,512]{1,0:T(4,128)} %leaf_assign.1, s32[1,128]{1,0:T(1,128)} %device_pick.1, s32[1,512]{1,0:T(1,128)} %device_assign.1, ...), custom_call_target="tpu_custom_call" | custom-call | flops 268435456 | bytes 1048576 | tf_op jit(solution)/shard_map/rise/pallas_call | solution.py:282
  8.5 1.2 %collective-permute-start.4 = (f32[96,128]{1,0:T(8,128)}, f32[96,128]{1,0:T(8,128)S(1)}, u32[]{:S(2)}, u32[]{:S(2)}) collective-permute-start(f32[96,128]{1,0:T(8,128)} %get-tuple-element.23), channel_id=1, source_target_pairs={{0,1},{1,0},{2,3},{3,2},{4,5},{5,4},{6,7},{7,6},{8,9},{9,8},{10,11... | collective-permute-start | bytes 147464 | tf_op jit(solution)/shard_map/ppermute | solution.py:29
  9.7 2.4 %collective-permute-done.4 = f32[96,128]{1,0:T(8,128)S(1)} collective-permute-done((f32[96,128]{1,0:T(8,128)}, f32[96,128]{1,0:T(8,128)S(1)}, u32[]{:S(2)}, u32[]{:S(2)}) %collective-permute-start.4) | collective-permute-done | bytes 49184 | tf_op jit(solution)/shard_map/ppermute | solution.py:29
  12.9 2.9 %collective-permute-done.5 = f32[96,128]{1,0:T(8,128)S(1)} collective-permute-done((f32[96,128]{1,0:T(8,128)S(1)}, f32[96,128]{1,0:T(8,128)S(1)}, u32[]{:S(2)}, u32[]{:S(2)}) %collective-permute-start.5) | collective-permute-done | bytes 49184 | tf_op jit(solution)/shard_map/ppermute | solution.py:29
  15.9 1.6 %collective-permute-start.6 = (f32[1,96,128]{2,1,0:T(8,128)S(1)}, f32[1,96,128]{2,1,0:T(8,128)S(1)}, u32[]{:S(2)}, u32[]{:S(2)}) collective-permute-start(f32[1,96,128]{2,1,0:T(8,128)S(1)} %add_bitcast_fusion), channel_id=1, source_target_pairs={{0,4},{4,0},{8,12},{12,8},{16,20},{20,16},{24,28},{28,24},{1,5},{5... | collective-permute-start | bytes 147464 | tf_op jit(solution)/shard_map/ppermute | solution.py:29
  18.4 1.2 %collective-permute-start.3 = (bf16[96,2048]{1,0:T(8,128)(2,1)}, bf16[96,2048]{1,0:T(8,128)(2,1)S(1)}, u32[]{:S(2)}, u32[]{:S(2)}) collective-permute-start(bf16[96,2048]{1,0:T(8,128)(2,1)} %get-tuple-element.29), channel_id=1, source_target_pairs={{0,1},{1,0},{2,3},{3,2},{4,5},{5,4},{6,7},{7,6},{8,9},{9,8},{10,11... | collective-permute-start | bytes 1179656 | tf_op jit(solution)/shard_map/ppermute | solution.py:29
  19.6 4.5 %own.1 = (bf16[2048,208]{1,0:T(8,128)(2,1)S(1)}, f32[32,2048]{1,0:T(8,128)S(1)}) custom-call(bf16[64,2048]{1,0:T(8,128)(2,1)} %points_ref.3, bf16[32,2048]{1,0:T(8,128)(2,1)} %values_ref.11), custom_call_target="tpu_custom_call" | custom-call | flops 4026531840 | bytes 2097152 | tf_op jit(solution)/shard_map/own/pallas_call | solution.py:296
  24.1 1.7 %collective-permute-start.7 = (f32[2,96,128]{2,1,0:T(8,128)S(1)}, f32[2,96,128]{2,1,0:T(8,128)S(1)}, u32[]{:S(2)}, u32[]{:S(2)}) collective-permute-start(f32[2,96,128]{2,1,0:T(8,128)S(1)} %pad_maximum_fusion.2), channel_id=1, source_target_pairs={{0,8},{4,12},{8,0},{12,4},{16,24},{20,28},{24,16},{28,20},{1,9},{5... | collective-permute-start | bytes 294920 | tf_op jit(solution)/shard_map/ppermute | solution.py:29
  26.5 2.1 %collective-permute-done.7 = f32[2,96,128]{2,1,0:T(8,128)S(1)} collective-permute-done((f32[2,96,128]{2,1,0:T(8,128)S(1)}, f32[2,96,128]{2,1,0:T(8,128)S(1)}, u32[]{:S(2)}, u32[]{:S(2)}) %collective-permute-start.7) | collective-permute-done | bytes 98336 | tf_op jit(solution)/shard_map/ppermute | solution.py:29
  28.6 2.4 %collective-permute-start.8 = (f32[4,96,128]{2,1,0:T(8,128)S(1)}, f32[4,96,128]{2,1,0:T(8,128)}, u32[]{:S(2)}, u32[]{:S(2)}) collective-permute-start(f32[4,96,128]{2,1,0:T(8,128)S(1)} %pad_maximum_fusion.1), channel_id=1, source_target_pairs={{0,16},{4,20},{8,24},{12,28},{16,0},{20,4},{24,8},{28,12},{1,17},{... | collective-permute-start | bytes 589832 | tf_op jit(solution)/shard_map/ppermute | solution.py:29
  31.2 1.2 %collective-permute-start.1 = (bf16[96,2048]{1,0:T(8,128)(2,1)}, bf16[96,2048]{1,0:T(8,128)(2,1)}, u32[]{:S(2)}, u32[]{:S(2)}) collective-permute-start(bf16[96,2048]{1,0:T(8,128)(2,1)} %get-tuple-element.30), channel_id=1, source_target_pairs={{0,3},{1,2},{2,1},{3,0},{4,7},{5,6},{6,5},{7,4},{8,11},{9,10},{10,... | collective-permute-start | bytes 1179656 | tf_op jit(solution)/shard_map/ppermute | solution.py:29
  32.4 6.7 %near1.1 = (f32[32,2048]{1,0:T(8,128)S(1)}, bf16[32,2048]{1,0:T(8,128)(2,1)}) custom-call(s32[2]{0:T(128)} %pad_add_fusion.1.where_ref, s32[1,4,12]{2,1,0:T(4,128)} %lower_ref.7, s32[1,4,12]{2,1,0:T(4,128)} %upper_ref.7, bf16[2048,208]{1,0:T(8,128)(2,1)S(1)} %get-tuple-element.17.rows_ref, ...), custom_call_target="tpu_custom_call", output_to_operand_aliasing={{0}: (6, {})} | custom-call | flops 4831838208 | bytes 2097152 | tf_op jit(solution)/shard_map/near1/pallas_call | solution.py:310
  39.0 10.4 %collective-permute-done.2.other_ref = bf16[96,2048]{1,0:T(8,128)(2,1)S(1)} collective-permute-done((bf16[96,2048]{1,0:T(8,128)(2,1)}, bf16[96,2048]{1,0:T(8,128)(2,1)S(1)}, u32[]{:S(2)}, u32[]{:S(2)}) %collective-permute-start.2) | collective-permute-done | bytes 393248 | tf_op jit(solution)/shard_map/ppermute | solution.py:29
  49.5 6.6 %near2.1 = (f32[32,2048]{1,0:T(8,128)S(1)}, bf16[32,2048]{1,0:T(8,128)(2,1)}) custom-call(s32[2]{0:T(128)} %pad_add_fusion.1.where_ref, s32[1,4,12]{2,1,0:T(4,128)} %lower_ref.7, s32[1,4,12]{2,1,0:T(4,128)} %upper_ref.7, bf16[2048,208]{1,0:T(8,128)(2,1)S(1)} %get-tuple-element.17.rows_ref, ...), custom_call_target="tpu_custom_call", output_to_operand_aliasing={{0}: (6, {})} | custom-call | flops 4831838208 | bytes 2097152 | tf_op jit(solution)/shard_map/near2/pallas_call | solution.py:310
  56.1 6.8 %near3.1 = (f32[32,2048]{1,0:T(8,128)S(1)}, bf16[32,2048]{1,0:T(8,128)(2,1)}) custom-call(s32[2]{0:T(128)} %pad_add_fusion.1.where_ref, s32[1,4,12]{2,1,0:T(4,128)} %lower_ref.7, s32[1,4,12]{2,1,0:T(4,128)} %upper_ref.7, bf16[2048,208]{1,0:T(8,128)(2,1)S(1)} %get-tuple-element.17.rows_ref, ...), custom_call_target="tpu_custom_call", output_to_operand_aliasing={{0}: (6, {})} | custom-call | flops 4831838208 | bytes 2097152 | tf_op jit(solution)/shard_map/near3/pallas_call | solution.py:310
  63.1 2.6 %collective-permute-start.9 = (bf16[32,2048]{1,0:T(8,128)(2,1)S(1)}, bf16[32,2048]{1,0:T(8,128)(2,1)S(1)}, u32[]{:S(2)}, u32[]{:S(2)}) collective-permute-start(bf16[32,2048]{1,0:T(8,128)(2,1)S(1)} %copy-done.2), channel_id=1, source_target_pairs={{0,1},{1,0},{2,3},{3,2},{4,5},{5,4},{6,7},{7,6},{8,9},{9,8},{10,11... | collective-permute-start | bytes 393224 | tf_op jit(solution)/shard_map/ppermute | solution.py:29
  65.6 6.6 %near0.1 = (f32[32,2048]{1,0:T(8,128)S(1)}, bf16[32,2048]{1,0:T(8,128)(2,1)}) custom-call(s32[2]{0:T(128)} %pad_add_fusion.1.where_ref, s32[1,4,12]{2,1,0:T(4,128)} %lower_ref.7, s32[1,4,12]{2,1,0:T(4,128)} %upper_ref.7, bf16[2048,208]{1,0:T(8,128)(2,1)S(1)} %get-tuple-element.17.rows_ref, ...), custom_call_target="tpu_custom_call", output_to_operand_aliasing={{0}: (6, {})} | custom-call | flops 4831838208 | bytes 2097152 | tf_op jit(solution)/shard_map/near0/pallas_call | solution.py:310
  73.3 5.6 %collective-permute-start.12 = (bf16[32,2048]{1,0:T(8,128)(2,1)S(1)}, bf16[32,2048]{1,0:T(8,128)(2,1)S(1)}, u32[]{:S(2)}, u32[]{:S(2)}) collective-permute-start(bf16[32,2048]{1,0:T(8,128)(2,1)S(1)} %fusion.7), channel_id=1, source_target_pairs={{0,4},{4,8},{8,12},{12,16},{16,20},{20,24},{24,28},{1,5},{5,9},{9,... | collective-permute-start | bytes 393224 | tf_op jit(solution)/shard_map/ppermute | solution.py:24
  78.9 1.7 %pad_maximum_fusion.roots_ref = f32[8,96,128]{2,1,0:T(8,128)} fusion(f32[4,96,128]{2,1,0:T(8,128)} %collective-permute-done.8, f32[2,96,128]{2,1,0:T(8,128)S(1)} %collective-permute-done.7, f32[1,96,128]{2,1,0:T(8,128)S(1)} %collective-permute-done.6, f32[1,96,128]{2,1,0:T(8,128)S(1)} %add_bitcast_fusion), kind=kLoop, calls=%fused_computation | loop fusion | flops 294912 | bytes 786432 | tf_op jit(solution)/shard_map/concatenate | solution.py:294
  80.6 2.4 %roots.1.root_ref = f32[32,128]{1,0:T(8,128)} custom-call(s32[2]{0:T(128)} %pad_add_fusion.1.where_ref, s32[1,8]{1,0:T(1,128)} %mask_ref.1, f32[8,96,128]{2,1,0:T(8,128)} %pad_maximum_fusion.roots_ref), custom_call_target="tpu_custom_call" | custom-call | flops 268435456 | bytes 1048576 | tf_op jit(solution)/shard_map/roots/pallas_call | solution.py:340
  83.0 1.8 %fall.1 = f32[32,2048]{1,0:T(8,128)} custom-call(f32[32,2048]{1,0:T(8,128)S(1)} %get-tuple-element.22.near_ref, f32[32,128]{1,0:T(8,128)} %roots.1.root_ref, bf16[128,2048]{1,0:T(8,128)(2,1)S(1)} %get-tuple-element.24.spread_ref), custom_call_target="tpu_custom_call" | custom-call | flops 67108864 | bytes 1048576 | tf_op jit(solution)/shard_map/fall/pallas_call | solution.py:348
  84.8 1.8 %fusion.3 = f32[32,2048]{1,0:T(8,128)} fusion(f32[32,2048]{1,0:T(8,128)} %fall.1, bf16[32,2048]{1,0:T(8,128)(2,1)S(1)} %collective-permute-done.9, bf16[32,2048]{1,0:T(8,128)(2,1)S(1)} %collective-permute-done.10, bf16[32,2048]{1,0:T(8,128)(2,1)S(1)} %collective-permute-done.11, bf16[32,2048]{1,0:T(8,128)(2,1)S(1)} %collective-permute-done.12, pred[]{:T(512)S(6)} %eq.4, ...), kind=kLoop, calls=%fused_computation.12 | loop fusion | flops 720896 | bytes 1048578 | tf_op jit(solution)/shard_map/add | solution.py:356
  (32 shorter events, 5.8 us)
Async XLA Ops:
  0.0 1.0 %copy-start = (bf16[32,2048]{1,0:T(8,128)(2,1)S(1)}, bf16[32,2048]{1,0:T(8,128)(2,1)}, u32[]{:S(2)}) copy-start(bf16[32,2048]{1,0:T(8,128)(2,1)} %values_ref.11) | copy-start | bytes 393220
  1.0 16.5 %collective-permute-start = (bf16[96,2048]{1,0:T(8,128)(2,1)S(1)}, bf16[96,2048]{1,0:T(8,128)(2,1)S(1)}, u32[]{:S(2)}, u32[]{:S(2)}) collective-permute-start(bf16[96,2048]{1,0:T(8,128)(2,1)S(1)} %constant_dynamic-update-slice_fusion), channel_id=1, source_target_pairs={{4,0},{8,4},{12,8},{16,12},{20,16},{24,20},{28,24},{5,1},{9,5},{13... | collective-permute-start | bytes 1179656 | tf_op jit(solution)/shard_map/ppermute | solution.py:24
  3.6 0.7 copy-start.1
  8.5 3.6 %collective-permute-start.4 = (f32[96,128]{1,0:T(8,128)}, f32[96,128]{1,0:T(8,128)S(1)}, u32[]{:S(2)}, u32[]{:S(2)}) collective-permute-start(f32[96,128]{1,0:T(8,128)} %get-tuple-element.23), channel_id=1, source_target_pairs={{0,1},{1,0},{2,3},{3,2},{4,5},{5,4},{6,7},{7,6},{8,9},{9,8},{10,11... | collective-permute-start | bytes 147464 | tf_op jit(solution)/shard_map/ppermute | solution.py:29
  12.9 2.9 %collective-permute-start.5 = (f32[96,128]{1,0:T(8,128)S(1)}, f32[96,128]{1,0:T(8,128)S(1)}, u32[]{:S(2)}, u32[]{:S(2)}) collective-permute-start(f32[96,128]{1,0:T(8,128)S(1)} %add.51), channel_id=1, source_target_pairs={{0,2},{1,3},{2,0},{3,1},{4,6},{5,7},{6,4},{7,5},{8,10},{9,11},{10,... | collective-permute-start | bytes 147464 | tf_op jit(solution)/shard_map/ppermute | solution.py:29
  15.9 8.2 %collective-permute-start.6 = (f32[1,96,128]{2,1,0:T(8,128)S(1)}, f32[1,96,128]{2,1,0:T(8,128)S(1)}, u32[]{:S(2)}, u32[]{:S(2)}) collective-permute-start(f32[1,96,128]{2,1,0:T(8,128)S(1)} %add_bitcast_fusion), channel_id=1, source_target_pairs={{0,4},{4,0},{8,12},{12,8},{16,20},{20,16},{24,28},{28,24},{1,5},{5... | collective-permute-start | bytes 147464 | tf_op jit(solution)/shard_map/ppermute | solution.py:29
  18.4 14.0 %collective-permute-start.3 = (bf16[96,2048]{1,0:T(8,128)(2,1)}, bf16[96,2048]{1,0:T(8,128)(2,1)S(1)}, u32[]{:S(2)}, u32[]{:S(2)}) collective-permute-start(bf16[96,2048]{1,0:T(8,128)(2,1)} %get-tuple-element.29), channel_id=1, source_target_pairs={{0,1},{1,0},{2,3},{3,2},{4,5},{5,4},{6,7},{7,6},{8,9},{9,8},{10,11... | collective-permute-start | bytes 1179656 | tf_op jit(solution)/shard_map/ppermute | solution.py:29
  24.1 4.4 %collective-permute-start.7 = (f32[2,96,128]{2,1,0:T(8,128)S(1)}, f32[2,96,128]{2,1,0:T(8,128)S(1)}, u32[]{:S(2)}, u32[]{:S(2)}) collective-permute-start(f32[2,96,128]{2,1,0:T(8,128)S(1)} %pad_maximum_fusion.2), channel_id=1, source_target_pairs={{0,8},{4,12},{8,0},{12,4},{16,24},{20,28},{24,16},{28,20},{1,9},{5... | collective-permute-start | bytes 294920 | tf_op jit(solution)/shard_map/ppermute | solution.py:29
  28.6 50.3 %collective-permute-start.8 = (f32[4,96,128]{2,1,0:T(8,128)S(1)}, f32[4,96,128]{2,1,0:T(8,128)}, u32[]{:S(2)}, u32[]{:S(2)}) collective-permute-start(f32[4,96,128]{2,1,0:T(8,128)S(1)} %pad_maximum_fusion.1), channel_id=1, source_target_pairs={{0,16},{4,20},{8,24},{12,28},{16,0},{20,4},{24,8},{28,12},{1,17},{... | collective-permute-start | bytes 589832 | tf_op jit(solution)/shard_map/ppermute | solution.py:29
  30.9 18.5 %collective-permute-start.2 = (bf16[96,2048]{1,0:T(8,128)(2,1)}, bf16[96,2048]{1,0:T(8,128)(2,1)S(1)}, u32[]{:S(2)}, u32[]{:S(2)}) collective-permute-start(bf16[96,2048]{1,0:T(8,128)(2,1)} %get-tuple-element.30), channel_id=1, source_target_pairs={{0,2},{1,3},{2,0},{3,1},{4,6},{5,7},{6,4},{7,5},{8,10},{9,11},{10,... | collective-permute-start | bytes 1179656 | tf_op jit(solution)/shard_map/ppermute | solution.py:29
  31.2 24.9 %collective-permute-start.1 = (bf16[96,2048]{1,0:T(8,128)(2,1)}, bf16[96,2048]{1,0:T(8,128)(2,1)}, u32[]{:S(2)}, u32[]{:S(2)}) collective-permute-start(bf16[96,2048]{1,0:T(8,128)(2,1)} %get-tuple-element.30), channel_id=1, source_target_pairs={{0,3},{1,2},{2,1},{3,0},{4,7},{5,6},{6,5},{7,4},{8,11},{9,10},{10,... | collective-permute-start | bytes 1179656 | tf_op jit(solution)/shard_map/ppermute | solution.py:29
  56.1 6.9 %copy-start.3 = (bf16[32,2048]{1,0:T(8,128)(2,1)S(1)}, bf16[32,2048]{1,0:T(8,128)(2,1)}, u32[]{:S(2)}) copy-start(bf16[32,2048]{1,0:T(8,128)(2,1)} %get-tuple-element.26) | copy-start | bytes 393220
  56.1 6.9 %copy-start.2 = (bf16[32,2048]{1,0:T(8,128)(2,1)S(1)}, bf16[32,2048]{1,0:T(8,128)(2,1)}, u32[]{:S(2)}) copy-start(bf16[32,2048]{1,0:T(8,128)(2,1)} %get-tuple-element.25) | copy-start | bytes 393220
  63.0 9.3 %collective-permute-start.11 = (bf16[32,2048]{1,0:T(8,128)(2,1)}, bf16[32,2048]{1,0:T(8,128)(2,1)S(1)}, u32[]{:S(2)}, u32[]{:S(2)}) collective-permute-start(bf16[32,2048]{1,0:T(8,128)(2,1)} %get-tuple-element.27), channel_id=1, source_target_pairs={{0,3},{1,2},{2,1},{3,0},{4,7},{5,6},{6,5},{7,4},{8,11},{9,10},{10,... | collective-permute-start | bytes 393224 | tf_op jit(solution)/shard_map/ppermute | solution.py:29
  63.0 9.3 %collective-permute-start.10 = (bf16[32,2048]{1,0:T(8,128)(2,1)S(1)}, bf16[32,2048]{1,0:T(8,128)(2,1)S(1)}, u32[]{:S(2)}, u32[]{:S(2)}) collective-permute-start(bf16[32,2048]{1,0:T(8,128)(2,1)S(1)} %copy-done.3), channel_id=1, source_target_pairs={{0,2},{1,3},{2,0},{3,1},{4,6},{5,7},{6,4},{7,5},{8,10},{9,11},{10,... | collective-permute-start | bytes 393224 | tf_op jit(solution)/shard_map/ppermute | solution.py:29
  63.1 9.2 %collective-permute-start.9 = (bf16[32,2048]{1,0:T(8,128)(2,1)S(1)}, bf16[32,2048]{1,0:T(8,128)(2,1)S(1)}, u32[]{:S(2)}, u32[]{:S(2)}) collective-permute-start(bf16[32,2048]{1,0:T(8,128)(2,1)S(1)} %copy-done.2), channel_id=1, source_target_pairs={{0,1},{1,0},{2,3},{3,2},{4,5},{5,4},{6,7},{7,6},{8,9},{9,8},{10,11... | collective-permute-start | bytes 393224 | tf_op jit(solution)/shard_map/ppermute | solution.py:29
  73.3 11.5 %collective-permute-start.12 = (bf16[32,2048]{1,0:T(8,128)(2,1)S(1)}, bf16[32,2048]{1,0:T(8,128)(2,1)S(1)}, u32[]{:S(2)}, u32[]{:S(2)}) collective-permute-start(bf16[32,2048]{1,0:T(8,128)(2,1)S(1)} %fusion.7), channel_id=1, source_target_pairs={{0,4},{4,8},{8,12},{12,16},{16,20},{20,24},{24,28},{1,5},{5,9},{9,... | collective-permute-start | bytes 393224 | tf_op jit(solution)/shard_map/ppermute | solution.py:24

commit v3 on v2

v3 whole, which is shorter than its diff:
```python
import functools
import math

import jax
import jax.numpy as jnp
from jax import lax
from jax.experimental import pallas as pl
from jax.experimental.pallas import tpu as pltpu
from jax.sharding import PartitionSpec as P


LPD = 4
SKEL = 128
KERNEL_RATE = 2.0
LOG2E = math.log2(math.e)
ROWS_AUG = 16
F32, BF16 = jnp.float32, jnp.bfloat16
VMEM = pl.BlockSpec(memory_space=pltpu.VMEM)


def passed_along(value, axis, steps):
    count = lax.axis_size(axis)
    first, last = (max(0, -steps), min(count, count - steps))
    pairs = [(source, source + steps) for source in range(first, last)]
    return lax.ppermute(value, axis, pairs)


def swapped(value, axis, mask):
    pairs = [(source, source ^ mask) for source in range(lax.axis_size(axis))]
    return lax.ppermute(value, axis, pairs)


def split3(value):
    first = value.astype(BF16)
    rest = value - first.astype(F32)
    second = rest.astype(BF16)
    third = (rest - second.astype(F32)).astype(BF16)
    return first, second, third


def norm_rows(points, scale, norms_first):
    wide = points.astype(F32)
    norm = -0.5 * scale * jnp.sum(wide * wide, axis=0, keepdims=True)
    row = lax.broadcasted_iota(jnp.int32, (ROWS_AUG, points.shape[1]), 0)
    start = 0 if norms_first else 3
    ones = (row >= 3 - start) & (row < 6 - start)
    rows = jnp.where(ones, 1.0, 0.0)
    for index, part in enumerate(split3(norm)):
        rows = jnp.where(row == start + index, part.astype(F32), rows)
    return rows.astype(BF16)


def source_rows(points, scale):
    parts = split3(points.astype(F32) * scale)
    return jnp.concatenate([*parts, norm_rows(points, scale, True)], 0).T


def target_columns(points, norms):
    return jnp.concatenate([points, points, points, norms], 0)


def tile_of(rows, points, norms):
    product = jnp.dot(rows, target_columns(points, norms), preferred_element_type=F32)
    return jnp.exp2(product).astype(BF16)


def dot_back(values, tile):
    return lax.dot_general(values, tile, (((1,), (1,)), ((), ())), preferred_element_type=F32)


def self_kernel(scale, leaf, own_ref, rows_ref, near_ref, norms_ref, tiles_ref):
    dim = own_ref.shape[0] - near_ref.shape[0]
    points_ref, values_ref = own_ref.at[:dim, :], own_ref.at[dim:, :]
    norms_ref[...] = norm_rows(points_ref[...], scale, False)
    at = [pl.ds(index * leaf, leaf) for index in range(LPD)]
    for index in range(LPD):
        rows_ref[at[index], :] = source_rows(points_ref[:, at[index]], scale)
    near_ref[...] = jnp.zeros_like(near_ref)

    def add(slot, low, high):
        near_ref[:, at[high]] += jnp.dot(
            values_ref[:, at[low]], tiles_ref[slot], preferred_element_type=F32
        )
        if low != high:
            near_ref[:, at[low]] += dot_back(values_ref[:, at[high]], tiles_ref[slot])

    pairs = [(low, high) for low in range(LPD) for high in range(low, LPD)]
    for slot, (low, high) in enumerate(pairs):
        tiles_ref[slot] = tile_of(
            rows_ref[at[low], :], points_ref[:, at[high]], norms_ref[:, at[high]]
        )
        if slot:
            add(slot - 1, *pairs[slot - 1])
    add(len(pairs) - 1, *pairs[-1])


def pair_kernel(
    scale,
    leaf,
    partner,
    group,
    lower_ref,
    upper_ref,
    rows_ref,
    own_ref,
    other_ref,
    near_in,
    near_ref,
    out_ref,
    norms_ref,
    upper_sum,
    tiles_ref,
):
    cols = near_ref.shape[0]
    dim = own_ref.shape[0] - cols
    reach, row_index = lax.axis_size("gy"), lax.axis_index("gy")
    offset = lax.rem((row_index ^ partner) - row_index + reach - 1, reach)
    lower, upper = (ref[0, pl.ds(offset, 1), :] for ref in (lower_ref, upper_ref))
    codes = jnp.where(lower >= 0, lower * LPD + upper, -1)
    upper_sum[...] = jnp.zeros_like(upper_sum)
    norms_ref[...] = norm_rows(other_ref[:dim, :], scale, False)

    def slot_of(index):
        code = codes[0, index]
        pair = jnp.maximum(code, 0)
        low = pl.multiple_of(lax.div(pair, LPD) * leaf, leaf)
        return code >= 0, low, pl.multiple_of(lax.rem(pair, LPD) * leaf, leaf)

    def add(slot, live, low, high):
        flag = jnp.where(live, 1.0, 0.0).astype(BF16)
        low_at, high_at = pl.ds(low, leaf), pl.ds(high, leaf)
        tile = tiles_ref[slot]
        upper_sum[:, high_at] += jnp.dot(
            own_ref[dim:, low_at] * flag, tile, preferred_element_type=F32
        )
        near_ref[:, low_at] += dot_back(other_ref[dim:, high_at] * flag, tile)

    def some_slots(slots):
        for index, (_, low, high) in enumerate(slots):
            tiles_ref[index] = tile_of(
                rows_ref[pl.ds(low, leaf), :],
                other_ref[:dim, pl.ds(high, leaf)],
                norms_ref[:, pl.ds(high, leaf)],
            )
            if index:
                add(index - 1, *slots[index - 1])
        add(group - 1, *slots[group - 1])

    for start in range(0, lower_ref.shape[2], group):
        slots = [slot_of(index) for index in range(start, start + group)]
        live = functools.reduce(jnp.logical_or, [slot[0] for slot in slots])
        pl.when(live)(functools.partial(some_slots, slots))
    out_ref[...] = upper_sum[...].astype(BF16)


def picked(index_row, count):
    wide = (count, index_row.shape[1])
    rows = lax.broadcasted_iota(jnp.int32, wide, 0)
    return jnp.where(rows == index_row, 1.0, 0.0).astype(BF16)


def flags_dot(left, right):
    return jnp.dot(left, right, preferred_element_type=F32).astype(BF16)


def rise_kernel(
    levels,
    leaf,
    dim,
    own_ref,
    leaf_pick,
    leaf_assign,
    device_pick,
    device_assign,
    node_pick,
    node_assign,
    share_ref,
    spread_ref,
):
    row_index = lax.axis_index("gy")
    picks = picked(device_pick[...], LPD * SKEL)
    assigns = picked(device_assign[...], SKEL)
    for level in range(1, levels + 1):
        heap = (1 << (levels - level)) - 1 + (row_index >> level)
        side = (row_index >> (level - 1)) & 1
        both = node_assign[heap]
        step_assign = jnp.where(side == 0, both[:, :SKEL], both[:, SKEL:])
        picks = flags_dot(picks, picked(node_pick[heap] - side * SKEL, SKEL))
        assigns = flags_dot(picked(step_assign, SKEL), assigns)
    root_points = jnp.zeros((dim, SKEL), F32)
    root_weights = jnp.zeros((own_ref.shape[0] - dim, SKEL), F32)
    for index in range(LPD):
        at = pl.ds(index * leaf, leaf)
        node = slice(index * SKEL, (index + 1) * SKEL)
        chosen = flags_dot(own_ref[:dim, at], picked(leaf_pick[index : index + 1, :], leaf))
        root_points += jnp.dot(chosen, picks[node], preferred_element_type=F32)
        spread = flags_dot(assigns[:, node], picked(leaf_assign[index : index + 1, :], SKEL))
        spread_ref[:, at] = spread
        root_weights += dot_back(own_ref[dim:, at], spread)
    share_ref[:dim, :] = root_points
    share_ref[dim:, :] = root_weights


def root_kernel(scale, mask_ref, *refs):
    parts, out_ref = refs[:-1], refs[-1]
    roots = [part[index] for part in parts for index in range(part.shape[0])]
    dim = roots[0].shape[0] - out_ref.shape[0]
    target = source_rows(roots[0][:dim].astype(BF16), scale)
    group = lax.broadcasted_iota(jnp.int32, mask_ref.shape, 1) ^ lax.axis_index("gx")
    weights = []
    for index in range(1, len(roots)):
        flag = jnp.sum(jnp.where(group == index, mask_ref[...], 0), axis=1, keepdims=True)
        weights.append(roots[index][dim:] * flag.astype(F32))
    source = jnp.concatenate([root[:dim].astype(BF16) for root in roots[1:]], 1)
    product = jnp.dot(
        target,
        target_columns(source, norm_rows(source, scale, False)),
        preferred_element_type=F32,
    )
    out_ref[...] = lax.dot_general(
        jnp.concatenate(weights, 1),
        jnp.exp2(product),
        (((1,), (1,)), ((), ())),
        preferred_element_type=F32,
        precision=lax.Precision.HIGHEST,
    )


def route_kernel(own_ref, ahead_ref, *out_refs):
    row_index = lax.axis_index("gy")
    for bit, out_ref in enumerate(out_refs):
        upper_side = (row_index >> bit) & 1 == 1

        @pl.when(upper_side)
        def _():
            out_ref[...] = own_ref[...]

        @pl.when(jnp.logical_not(upper_side))
        def _():
            out_ref[...] = ahead_ref[...]


def add_kernel(left_ref, right_ref, out_ref):
    out_ref[...] = (left_ref[...] + right_ref[...]).reshape(out_ref.shape)


def join_kernel(*refs):
    parts, out_ref = refs[:-1], refs[-1]
    start = 0
    for part in parts:
        out_ref[pl.ds(start, part.shape[0])] = part[...]
        start += part.shape[0]


def onward_kernel(partners, *refs):
    row_index = lax.axis_index("gy")
    total = refs[0][...].astype(F32)
    for partner, ref in zip(partners, refs[1:-1]):
        lower_side = (row_index >> (partner.bit_length() - 1)) & 1 == 0
        total += ref[...].astype(F32) * jnp.where(lower_side, 1.0, 0.0)
    refs[-1][...] = total.astype(BF16)


def fall_kernel(partners, near_ref, root_ref, spread_ref, *refs):
    row_index = lax.axis_index("gy")
    total = near_ref[...]
    for part in split3(root_ref[...]):
        total += jnp.dot(part, spread_ref[...], preferred_element_type=F32)
    for partner, ref in zip(partners, refs[:-1]):
        upper_side = (row_index >> (partner.bit_length() - 1)) & 1 == 1
        total += ref[...].astype(F32) * jnp.where(upper_side, 1.0, 0.0)
    refs[-1][...] = total


def last_kernel(local_ref, *refs):
    total = local_ref[...]
    for ref in refs[:-1]:
        total += ref[...].astype(F32)
    refs[-1][...] = total


def shape(*dims, dtype=F32):
    return jax.ShapeDtypeStruct(dims, dtype)


def kept(*dims, dtype=F32):
    return pltpu.VMEM(dims, dtype)


def run(kernel, outs, *args, flops=2**20, memory=4, scratch=(), aliases=None):
    many = isinstance(outs, tuple)
    return pl.pallas_call(
        kernel,
        out_shape=outs,
        in_specs=[VMEM] * len(args),
        out_specs=(VMEM,) * len(outs) if many else VMEM,
        scratch_shapes=list(scratch),
        input_output_aliases=aliases or {},
        cost_estimate=pl.CostEstimate(flops=flops, bytes_accessed=2**16, transcendentals=0),
        compiler_params=pltpu.CompilerParams(vmem_limit_bytes=memory * 2**20),
    )(*[pltpu.with_memory_space_constraint(arg, pltpu.VMEM) for arg in args])


def landing(partner, back):
    reach, count = lax.axis_size("gy"), lax.axis_size("gx") * lax.axis_size("gy")
    pairs = []
    for source in range(count):
        row = source % reach
        step = ((row ^ partner) - row - 1) % reach + 1
        if source + step < count:
            pairs.append((source, source + step))
    return lax.ppermute(back, ("gx", "gy"), pairs)


def on_device(
    points,
    vectors,
    leaf_pick,
    leaf_assign,
    device_pick,
    device_assign,
    node_pick,
    node_assign,
    far_mask,
    near_lower,
    near_upper,
):
    dim, device_cols = points.shape
    cols = vectors.shape[0]
    leaf = device_cols // LPD
    scale = 2.0 * KERNEL_RATE / dim * LOG2E
    width = 3 * dim + ROWS_AUG
    gx_count, reach = lax.axis_size("gx"), lax.axis_size("gy")
    levels = reach.bit_length() - 1
    slots = near_lower.shape[2]
    group = next(size for size in (4, 3, 2, 1) if slots % size == 0)
    tile_flops = 2 * leaf * leaf * (256 + 2 * 256)
    block = kept(dim + cols, device_cols, dtype=BF16)
    root_shape = (dim + cols, SKEL)

    packed = jnp.concatenate([points, vectors], 0)
    ahead = passed_along(packed, "gx", -1)

    share, spread = run(
        functools.partial(rise_kernel, levels, leaf, dim),
        (kept(*root_shape), kept(SKEL, device_cols, dtype=BF16)),
        packed,
        leaf_pick,
        leaf_assign,
        device_pick,
        device_assign,
        jnp.transpose(node_pick, (1, 0, 2)),
        jnp.transpose(node_assign, (1, 0, 2)),
        flops=2**29,
        memory=6,
    )
    for bit in range(levels):
        outs = kept(*root_shape) if bit + 1 < levels else kept(1, *root_shape)
        share = run(add_kernel, outs, share, swapped(share, "gy", 1 << bit))
    roots, sent = [share], share
    for bit in range(gx_count.bit_length() - 1):
        if bit:
            sent = run(join_kernel, kept(1 << bit, *root_shape), *roots)
        roots.append(swapped(sent, "gx", 1 << bit))

    rows, near = run(
        functools.partial(self_kernel, scale, leaf),
        (kept(device_cols, width, dtype=BF16), kept(cols, device_cols)),
        packed,
        flops=10 * tile_flops,
        memory=12,
        scratch=[
            pltpu.VMEM((ROWS_AUG, device_cols), BF16),
            pltpu.VMEM((LPD * (LPD + 1) // 2, leaf, leaf), BF16),
        ],
    )

    def meet(partner, other, near):
        return run(
            functools.partial(pair_kernel, scale, leaf, partner, group),
            (kept(cols, device_cols), kept(cols, device_cols, dtype=BF16)),
            near_lower,
            near_upper,
            rows,
            packed,
            other,
            near,
            flops=slots * tile_flops,
            memory=10,
            scratch=[
                pltpu.VMEM((ROWS_AUG, device_cols), BF16),
                pltpu.VMEM((cols, device_cols), F32),
                pltpu.VMEM((group, leaf, leaf), BF16),
            ],
            aliases={5: 0},
        )

    payloads = run(route_kernel, (block,) * levels, packed, ahead)
    others = [ahead]
    for partner in range(1, reach):
        others.append(swapped(payloads[partner.bit_length() - 1], "gy", partner))
    near, first_upper = meet(0, ahead, near)
    partners, backs = list(range(1, reach - 1)), []
    for partner in partners:
        near, upper = meet(partner, others[partner], near)
        backs.append(swapped(upper, "gy", partner))
    near, upper = meet(reach - 1, others[reach - 1], near)
    direct = landing(reach - 1, upper)
    onward = run(
        functools.partial(onward_kernel, partners),
        kept(cols, device_cols, dtype=BF16),
        first_upper,
        *backs,
    )
    landed = passed_along(onward, "gx", 1)
    root = run(
        functools.partial(root_kernel, scale), kept(cols, SKEL), far_mask, *roots, flops=2**28
    )
    local = run(
        functools.partial(fall_kernel, partners),
        kept(cols, device_cols),
        near,
        root,
        spread,
        *backs,
        flops=2**26,
    )
    return run(last_kernel, shape(cols, device_cols), local, landed, direct)


def solution(mesh):
    placed = (
        P(None, ("gx", "gy")),
        P(None, ("gx", "gy")),
        P(("gx", "gy"), None),
        P(("gx", "gy"), None),
        P(("gx", "gy"), None),
        P(("gx", "gy"), None),
        P("gx", None, None),
        P("gx", None, None),
        P("gx", None),
        P(("gx", "gy"), None, None),
        P(("gx", "gy"), None, None),
    )


    return jax.shard_map(
        on_device, mesh=mesh, in_specs=placed, out_specs=P(None, ("gx", "gy")), check_vma=False
    )
```

time: 87.5 us -> 73 us (0.83)
  the two profiles are of different devices: /device:TPU:5 before, /device:TPU:18 now
where the time goes in v3:
time: 73 us; the launch traced here: 72.7 us
  Pallas kernels  28.2 us (39%)
  waiting for transfers between devices  25.1 us (34%)
  starting transfers between devices  17.3 us (24%)
  local copies, waits for them, and re-layouts  1.72 us (2%)
    pallas_call x15, Pallas kernels, run(): pl.pallas_call(kernel, out_shape=outs, in_specs=[VMEM] * len(args), out_s...  28.2 us
    ppermute x10, waiting for transfers between devices, swapped(): return lax.ppermute(value, axis, pairs)  22 us
    ppermute x10, starting transfers between devices, swapped(): return lax.ppermute(value, axis, pairs)  9.6 us
    ppermute x2, starting transfers between devices, passed_along(): return lax.ppermute(value, axis, pairs)  4.37 us
    ppermute x1, starting transfers between devices, landing(): return lax.ppermute(back, ('gx', 'gy'), pairs)  3.35 us
    unnamed x21, local copies, waits for them, and re-layouts  1.71 us
    ppermute x2, waiting for transfers between devices, passed_along(): return lax.ppermute(value, axis, pairs)  1.68 us
    ppermute x1, waiting for transfers between devices, landing(): return lax.ppermute(back, ('gx', 'gy'), pairs)  1.47 us
  transfers between devices with their start and end apart: 13, of which 6 were waited for; matrix products, arithmetic and copies ran while one was open for 0% of the time, Pallas kernels for 36%

profile of v3, /device:TPU:18, one launch (start us, length us, event | category | flops | bytes accessed | tf_op | source)
XLA Modules:
  0.0 72.7 jit_solution(7338668144916982431)
XLA Ops:
  0.0 1.0 %constant_dynamic-update-slice_fusion.1 = bf16[96,2048]{1,0:T(8,128)(2,1)S(1)} fusion(bf16[64,2048]{1,0:T(8,128)(2,1)} %param.11), kind=kLoop, calls=%fused_computation.1 | loop fusion | bytes 524288
  1.1 0.6 copy-done
  1.8 1.2 %shard_map.115 = (f32[96,128]{1,0:T(8,128)S(1)}, bf16[128,2048]{1,0:T(8,128)(2,1)S(1)}) custom-call(bf16[96,2048]{1,0:T(8,128)(2,1)S(1)} %constant_dynamic-update-slice_fusion.own_ref, s32[4,128]{1,0:T(4,128)S(1)} %copy-done.2, s32[4,512]{1,0:T(4,128)S(1)} %copy-done, s32[1,128]{1,0:T(1,128)S(1)} %copy-done.7, s32[1,512]{1,0:T(1,128)S(1)} %copy-done.3, ...), custom_call_target="tpu_custom_call" | custom-call | flops 536870912 | bytes 65536 | tf_op jit(solution)/shard_map/pallas_call | solution.py:292
  3.6 3.6 %collective-permute-done.4.right_ref = f32[96,128]{1,0:T(8,128)S(1)} collective-permute-done((f32[96,128]{1,0:T(8,128)S(1)}, f32[96,128]{1,0:T(8,128)S(1)}, u32[]{:S(2)}, u32[]{:S(2)}) %collective-permute-start.4) | collective-permute-done | bytes 49184 | tf_op jit(solution)/shard_map/ppermute | solution.py:30
  7.1 1.6 %collective-permute-start.5 = (f32[96,128]{1,0:T(8,128)S(1)}, f32[96,128]{1,0:T(8,128)S(1)}, u32[]{:S(2)}, u32[]{:S(2)}) collective-permute-start(f32[96,128]{1,0:T(8,128)S(1)} %shard_map.116.left_ref), channel_id=1, source_target_pairs={{0,2},{1,3},{2,0},{3,1},{4,6},{5,7},{6,4},{7,5},{8,10},{9,11},{10,... | collective-permute-start | bytes 147464 | tf_op jit(solution)/shard_map/ppermute | solution.py:30
  8.7 2.6 %collective-permute-done.5.right_ref = f32[96,128]{1,0:T(8,128)S(1)} collective-permute-done((f32[96,128]{1,0:T(8,128)S(1)}, f32[96,128]{1,0:T(8,128)S(1)}, u32[]{:S(2)}, u32[]{:S(2)}) %collective-permute-start.5) | collective-permute-done | bytes 49184 | tf_op jit(solution)/shard_map/ppermute | solution.py:30
  11.3 2.4 %collective-permute-start = (bf16[96,2048]{1,0:T(8,128)(2,1)S(1)}, bf16[96,2048]{1,0:T(8,128)(2,1)S(1)}, u32[]{:S(2)}, u32[]{:S(2)}) collective-permute-start(bf16[96,2048]{1,0:T(8,128)(2,1)S(1)} %constant_dynamic-update-slice_fusion.own_ref), channel_id=1, source_target_pairs={{4,0},{8,4},{12,8},{16,12},{20,16},{24,20},{28,24},{5,1},{9,5},{13... | collective-permute-start | bytes 1179656 | tf_op jit(solution)/shard_map/ppermute | solution.py:25
  13.8 1.6 %collective-permute-start.7 = (f32[2,96,128]{2,1,0:T(8,128)S(1)}, f32[2,96,128]{2,1,0:T(8,128)S(1)}, u32[]{:S(2)}, u32[]{:S(2)}) collective-permute-start(f32[2,96,128]{2,1,0:T(8,128)S(1)} %shard_map.118), channel_id=1, source_target_pairs={{0,8},{4,12},{8,0},{12,4},{16,24},{20,28},{24,16},{28,20},{1,9},{5... | collective-permute-start | bytes 294920 | tf_op jit(solution)/shard_map/ppermute | solution.py:30
  15.5 3.5 %shard_map.109 = (bf16[2048,208]{1,0:T(8,128)(2,1)S(1)}, f32[32,2048]{1,0:T(8,128)S(1)}) custom-call(bf16[96,2048]{1,0:T(8,128)(2,1)S(1)} %constant_dynamic-update-slice_fusion.own_ref), custom_call_target="tpu_custom_call" | custom-call | flops 4026531840 | bytes 65536 | tf_op jit(solution)/shard_map/pallas_call | solution.py:292
  18.9 6.0 %collective-permute-done.7.refs_2_ = f32[2,96,128]{2,1,0:T(8,128)S(1)} collective-permute-done((f32[2,96,128]{2,1,0:T(8,128)S(1)}, f32[2,96,128]{2,1,0:T(8,128)S(1)}, u32[]{:S(2)}, u32[]{:S(2)}) %collective-permute-start.7) | collective-permute-done | bytes 98336 | tf_op jit(solution)/shard_map/ppermute | solution.py:30
  25.1 1.6 %collective-permute-start.2 = (bf16[96,2048]{1,0:T(8,128)(2,1)S(1)}, bf16[96,2048]{1,0:T(8,128)(2,1)S(1)}, u32[]{:S(2)}, u32[]{:S(2)}) collective-permute-start(bf16[96,2048]{1,0:T(8,128)(2,1)S(1)} %get-tuple-element.20), channel_id=1, source_target_pairs={{0,2},{1,3},{2,0},{3,1},{4,6},{5,7},{6,4},{7,5},{8,10},{9,11},{10,... | collective-permute-start | bytes 1179656 | tf_op jit(solution)/shard_map/ppermute | solution.py:30
  27.1 1.6 %collective-permute-start.3 = (bf16[96,2048]{1,0:T(8,128)(2,1)S(1)}, bf16[96,2048]{1,0:T(8,128)(2,1)S(1)}, u32[]{:S(2)}, u32[]{:S(2)}) collective-permute-start(bf16[96,2048]{1,0:T(8,128)(2,1)S(1)} %get-tuple-element.21), channel_id=1, source_target_pairs={{0,1},{1,0},{2,3},{3,2},{4,5},{5,4},{6,7},{7,6},{8,9},{9,8},{10,11... | collective-permute-start | bytes 1179656 | tf_op jit(solution)/shard_map/ppermute | solution.py:30
  28.6 5.3 %shard_map.111 = (f32[32,2048]{1,0:T(8,128)S(1)}, bf16[32,2048]{1,0:T(8,128)(2,1)S(1)}) custom-call(s32[1,4,12]{2,1,0:T(4,128)S(1)} %copy-done.4, s32[1,4,12]{2,1,0:T(4,128)S(1)} %copy-done.5, bf16[2048,208]{1,0:T(8,128)(2,1)S(1)} %get-tuple-element.19.rows_ref, ...), custom_call_target="tpu_custom_call", output_to_operand_aliasing={{0}: (5, {})} | custom-call | flops 4831838208 | bytes 65536 | tf_op jit(solution)/shard_map/pallas_call | solution.py:292
  34.0 9.9 %collective-permute-done.3.other_ref = bf16[96,2048]{1,0:T(8,128)(2,1)S(1)} collective-permute-done((bf16[96,2048]{1,0:T(8,128)(2,1)S(1)}, bf16[96,2048]{1,0:T(8,128)(2,1)S(1)}, u32[]{:S(2)}, u32[]{:S(2)}) %collective-permute-start.3) | collective-permute-done | bytes 393248 | tf_op jit(solution)/shard_map/ppermute | solution.py:30
  43.8 5.3 %shard_map.112 = (f32[32,2048]{1,0:T(8,128)S(1)}, bf16[32,2048]{1,0:T(8,128)(2,1)S(1)}) custom-call(s32[1,4,12]{2,1,0:T(4,128)S(1)} %copy-done.4, s32[1,4,12]{2,1,0:T(4,128)S(1)} %copy-done.5, bf16[2048,208]{1,0:T(8,128)(2,1)S(1)} %get-tuple-element.19.rows_ref, ...), custom_call_target="tpu_custom_call", output_to_operand_aliasing={{0}: (5, {})} | custom-call | flops 4831838208 | bytes 65536 | tf_op jit(solution)/shard_map/pallas_call | solution.py:292
  49.2 5.5 %shard_map.113 = (f32[32,2048]{1,0:T(8,128)S(1)}, bf16[32,2048]{1,0:T(8,128)(2,1)S(1)}) custom-call(s32[1,4,12]{2,1,0:T(4,128)S(1)} %copy-done.4, s32[1,4,12]{2,1,0:T(4,128)S(1)} %copy-done.5, bf16[2048,208]{1,0:T(8,128)(2,1)S(1)} %get-tuple-element.19.rows_ref, ...), custom_call_target="tpu_custom_call", output_to_operand_aliasing={{0}: (5, {})} | custom-call | flops 4831838208 | bytes 65536 | tf_op jit(solution)/shard_map/pallas_call | solution.py:292
  54.7 1.6 %collective-permute-start.10 = (bf16[32,2048]{1,0:T(8,128)(2,1)S(1)}, bf16[32,2048]{1,0:T(8,128)(2,1)S(1)}, u32[]{:S(2)}, u32[]{:S(2)}) collective-permute-start(bf16[32,2048]{1,0:T(8,128)(2,1)S(1)} %get-tuple-element.30), channel_id=1, source_target_pairs={{0,2},{1,3},{2,0},{3,1},{4,6},{5,7},{6,4},{7,5},{8,10},{9,11},{10,... | collective-permute-start | bytes 393224 | tf_op jit(solution)/shard_map/ppermute | solution.py:30
  56.8 5.3 %shard_map.114 = (f32[32,2048]{1,0:T(8,128)S(1)}, bf16[32,2048]{1,0:T(8,128)(2,1)S(1)}) custom-call(s32[1,4,12]{2,1,0:T(4,128)S(1)} %copy-done.4, s32[1,4,12]{2,1,0:T(4,128)S(1)} %copy-done.5, bf16[2048,208]{1,0:T(8,128)(2,1)S(1)} %get-tuple-element.19.rows_ref, ...), custom_call_target="tpu_custom_call", output_to_operand_aliasing={{0}: (5, {})} | custom-call | flops 4831838208 | bytes 65536 | tf_op jit(solution)/shard_map/pallas_call | solution.py:292
  62.2 3.4 %collective-permute-start.12 = (bf16[32,2048]{1,0:T(8,128)(2,1)S(1)}, bf16[32,2048]{1,0:T(8,128)(2,1)S(1)}, u32[]{:S(2)}, u32[]{:S(2)}) collective-permute-start(bf16[32,2048]{1,0:T(8,128)(2,1)S(1)} %get-tuple-element.32), channel_id=1, source_target_pairs={{0,3},{1,2},{2,5},{3,4},{4,7},{5,6},{6,9},{7,8},{8,11},{9,10},{10,... | collective-permute-start | bytes 393224 | tf_op jit(solution)/shard_map/ppermute | solution.py:312
  65.7 1.9 %collective-permute-start.11 = (bf16[32,2048]{1,0:T(8,128)(2,1)S(1)}, bf16[32,2048]{1,0:T(8,128)(2,1)S(1)}, u32[]{:S(2)}, u32[]{:S(2)}) collective-permute-start(bf16[32,2048]{1,0:T(8,128)(2,1)S(1)} %shard_map.122), channel_id=1, source_target_pairs={{0,4},{4,8},{8,12},{12,16},{16,20},{20,24},{24,28},{1,5},{5,9},{9,... | collective-permute-start | bytes 393224 | tf_op jit(solution)/shard_map/ppermute | solution.py:25
  67.6 0.8 %shard_map.120.root_ref = f32[32,128]{1,0:T(8,128)S(1)} custom-call(s32[1,8]{1,0:T(1,128)S(1)} %copy-done.8, f32[1,96,128]{2,1,0:T(8,128)S(1)} %shard_map.117.refs_0_, f32[1,96,128]{2,1,0:T(8,128)S(1)} %collective-permute-done.6.refs_1_, f32[2,96,128]{2,1,0:T(8,128)S(1)} %collective-permute-done.7.refs_2_, f32[4,96,128]{2,1,0:T(8,128)S(1)} %collective-permute-done.8.refs_3_), custom_call_target="tpu_custom_call" | custom-call | flops 268435456 | bytes 65536 | tf_op jit(solution)/shard_map/pallas_call | solution.py:292
  68.8 1.5 %collective-permute-done.12.refs_1_ = bf16[32,2048]{1,0:T(8,128)(2,1)S(1)} collective-permute-done((bf16[32,2048]{1,0:T(8,128)(2,1)S(1)}, bf16[32,2048]{1,0:T(8,128)(2,1)S(1)}, u32[]{:S(2)}, u32[]{:S(2)}) %collective-permute-start.12) | collective-permute-done | bytes 131104 | tf_op jit(solution)/shard_map/ppermute | solution.py:312
  70.3 1.7 %collective-permute-done.11.refs_0_ = bf16[32,2048]{1,0:T(8,128)(2,1)S(1)} collective-permute-done((bf16[32,2048]{1,0:T(8,128)(2,1)S(1)}, bf16[32,2048]{1,0:T(8,128)(2,1)S(1)}, u32[]{:S(2)}, u32[]{:S(2)}) %collective-permute-start.11) | collective-permute-done | bytes 131104 | tf_op jit(solution)/shard_map/ppermute | solution.py:25
  71.9 0.7 %shard_map.123 = f32[32,2048]{1,0:T(8,128)} custom-call(f32[32,2048]{1,0:T(8,128)S(1)} %shard_map.121.local_ref, bf16[32,2048]{1,0:T(8,128)(2,1)S(1)} %collective-permute-done.11.refs_0_, bf16[32,2048]{1,0:T(8,128)(2,1)S(1)} %collective-permute-done.12.refs_1_), custom_call_target="tpu_custom_call" | custom-call | flops 1048576 | bytes 65536 | tf_op jit(solution)/shard_map/pallas_call | solution.py:292
  (39 shorter events, 2.3 us)
Async XLA Ops:
  0.0 1.0 %copy-start.9 = (bf16[32,2048]{1,0:T(8,128)(2,1)S(1)}, bf16[32,2048]{1,0:T(8,128)(2,1)}, u32[]{:S(2)}) copy-start(bf16[32,2048]{1,0:T(8,128)(2,1)} %param.12) | copy-start | bytes 393220
  1.0 0.7 copy-start
  1.0 0.7 copy-start.2
  1.0 0.7 copy-start.3
  1.1 0.7 copy-start.6
  1.1 0.7 copy-start.1
  1.1 0.7 copy-start.7
  3.0 4.1 %collective-permute-start.4 = (f32[96,128]{1,0:T(8,128)S(1)}, f32[96,128]{1,0:T(8,128)S(1)}, u32[]{:S(2)}, u32[]{:S(2)}) collective-permute-start(f32[96,128]{1,0:T(8,128)S(1)} %get-tuple-element.27.left_ref), channel_id=1, source_target_pairs={{0,1},{1,0},{2,3},{3,2},{4,5},{5,4},{6,7},{7,6},{8,9},{9,8},{10,11... | collective-permute-start | bytes 147464 | tf_op jit(solution)/shard_map/ppermute | solution.py:30
  7.1 4.2 %collective-permute-start.5 = (f32[96,128]{1,0:T(8,128)S(1)}, f32[96,128]{1,0:T(8,128)S(1)}, u32[]{:S(2)}, u32[]{:S(2)}) collective-permute-start(f32[96,128]{1,0:T(8,128)S(1)} %shard_map.116.left_ref), channel_id=1, source_target_pairs={{0,2},{1,3},{2,0},{3,1},{4,6},{5,7},{6,4},{7,5},{8,10},{9,11},{10,... | collective-permute-start | bytes 147464 | tf_op jit(solution)/shard_map/ppermute | solution.py:30
  11.3 2.5 %collective-permute-start.6 = (f32[1,96,128]{2,1,0:T(8,128)S(1)}, f32[1,96,128]{2,1,0:T(8,128)S(1)}, u32[]{:S(2)}, u32[]{:S(2)}) collective-permute-start(f32[1,96,128]{2,1,0:T(8,128)S(1)} %shard_map.117.refs_0_), channel_id=1, source_target_pairs={{0,4},{4,0},{8,12},{12,8},{16,20},{20,16},{24,28},{28,24},{1,5},{5... | collective-permute-start | bytes 147464 | tf_op jit(solution)/shard_map/ppermute | solution.py:30
  11.3 13.6 %collective-permute-start = (bf16[96,2048]{1,0:T(8,128)(2,1)S(1)}, bf16[96,2048]{1,0:T(8,128)(2,1)S(1)}, u32[]{:S(2)}, u32[]{:S(2)}) collective-permute-start(bf16[96,2048]{1,0:T(8,128)(2,1)S(1)} %constant_dynamic-update-slice_fusion.own_ref), channel_id=1, source_target_pairs={{4,0},{8,4},{12,8},{16,12},{20,16},{24,20},{28,24},{5,1},{9,5},{13... | collective-permute-start | bytes 1179656 | tf_op jit(solution)/shard_map/ppermute | solution.py:25
  13.8 11.1 %collective-permute-start.7 = (f32[2,96,128]{2,1,0:T(8,128)S(1)}, f32[2,96,128]{2,1,0:T(8,128)S(1)}, u32[]{:S(2)}, u32[]{:S(2)}) collective-permute-start(f32[2,96,128]{2,1,0:T(8,128)S(1)} %shard_map.118), channel_id=1, source_target_pairs={{0,8},{4,12},{8,0},{12,4},{16,24},{20,28},{24,16},{28,20},{1,9},{5... | collective-permute-start | bytes 294920 | tf_op jit(solution)/shard_map/ppermute | solution.py:30
  24.9 42.7 %collective-permute-start.8 = (f32[4,96,128]{2,1,0:T(8,128)S(1)}, f32[4,96,128]{2,1,0:T(8,128)S(1)}, u32[]{:S(2)}, u32[]{:S(2)}) collective-permute-start(f32[4,96,128]{2,1,0:T(8,128)S(1)} %shard_map.119), channel_id=1, source_target_pairs={{0,16},{4,20},{8,24},{12,28},{16,0},{20,4},{24,8},{28,12},{1,17},{... | collective-permute-start | bytes 589832 | tf_op jit(solution)/shard_map/ppermute | solution.py:30
  25.1 24.1 %collective-permute-start.2 = (bf16[96,2048]{1,0:T(8,128)(2,1)S(1)}, bf16[96,2048]{1,0:T(8,128)(2,1)S(1)}, u32[]{:S(2)}, u32[]{:S(2)}) collective-permute-start(bf16[96,2048]{1,0:T(8,128)(2,1)S(1)} %get-tuple-element.20), channel_id=1, source_target_pairs={{0,2},{1,3},{2,0},{3,1},{4,6},{5,7},{6,4},{7,5},{8,10},{9,11},{10,... | collective-permute-start | bytes 1179656 | tf_op jit(solution)/shard_map/ppermute | solution.py:30
  26.7 30.2 %collective-permute-start.1 = (bf16[96,2048]{1,0:T(8,128)(2,1)S(1)}, bf16[96,2048]{1,0:T(8,128)(2,1)S(1)}, u32[]{:S(2)}, u32[]{:S(2)}) collective-permute-start(bf16[96,2048]{1,0:T(8,128)(2,1)S(1)} %get-tuple-element.20), channel_id=1, source_target_pairs={{0,3},{1,2},{2,1},{3,0},{4,7},{5,6},{6,5},{7,4},{8,11},{9,10},{10,... | collective-permute-start | bytes 1179656 | tf_op jit(solution)/shard_map/ppermute | solution.py:30
  27.1 1.6 %copy-start.5 = (s32[1,4,12]{2,1,0:T(4,128)S(1)}, s32[1,4,12]{2,1,0:T(4,128)}, u32[]{:S(2)}) copy-start(s32[1,4,12]{2,1,0:T(4,128)} %upper_ref.7) | copy-start | bytes 580
  27.1 1.6 %copy-start.4 = (s32[1,4,12]{2,1,0:T(4,128)S(1)}, s32[1,4,12]{2,1,0:T(4,128)}, u32[]{:S(2)}) copy-start(s32[1,4,12]{2,1,0:T(4,128)} %lower_ref.7) | copy-start | bytes 580
  27.1 16.8 %collective-permute-start.3 = (bf16[96,2048]{1,0:T(8,128)(2,1)S(1)}, bf16[96,2048]{1,0:T(8,128)(2,1)S(1)}, u32[]{:S(2)}, u32[]{:S(2)}) collective-permute-start(bf16[96,2048]{1,0:T(8,128)(2,1)S(1)} %get-tuple-element.21), channel_id=1, source_target_pairs={{0,1},{1,0},{2,3},{3,2},{4,5},{5,4},{6,7},{7,6},{8,9},{9,8},{10,11... | collective-permute-start | bytes 1179656 | tf_op jit(solution)/shard_map/ppermute | solution.py:30
  54.7 10.8 %collective-permute-start.10 = (bf16[32,2048]{1,0:T(8,128)(2,1)S(1)}, bf16[32,2048]{1,0:T(8,128)(2,1)S(1)}, u32[]{:S(2)}, u32[]{:S(2)}) collective-permute-start(bf16[32,2048]{1,0:T(8,128)(2,1)S(1)} %get-tuple-element.30), channel_id=1, source_target_pairs={{0,2},{1,3},{2,0},{3,1},{4,6},{5,7},{6,4},{7,5},{8,10},{9,11},{10,... | collective-permute-start | bytes 393224 | tf_op jit(solution)/shard_map/ppermute | solution.py:30
  56.3 9.3 %collective-permute-start.9 = (bf16[32,2048]{1,0:T(8,128)(2,1)S(1)}, bf16[32,2048]{1,0:T(8,128)(2,1)S(1)}, u32[]{:S(2)}, u32[]{:S(2)}) collective-permute-start(bf16[32,2048]{1,0:T(8,128)(2,1)S(1)} %get-tuple-element.29), channel_id=1, source_target_pairs={{0,1},{1,0},{2,3},{3,2},{4,5},{5,4},{6,7},{7,6},{8,9},{9,8},{10,11... | collective-permute-start | bytes 393224 | tf_op jit(solution)/shard_map/ppermute | solution.py:30
  62.2 8.1 %collective-permute-start.12 = (bf16[32,2048]{1,0:T(8,128)(2,1)S(1)}, bf16[32,2048]{1,0:T(8,128)(2,1)S(1)}, u32[]{:S(2)}, u32[]{:S(2)}) collective-permute-start(bf16[32,2048]{1,0:T(8,128)(2,1)S(1)} %get-tuple-element.32), channel_id=1, source_target_pairs={{0,3},{1,2},{2,5},{3,4},{4,7},{5,6},{6,9},{7,8},{8,11},{9,10},{10,... | collective-permute-start | bytes 393224 | tf_op jit(solution)/shard_map/ppermute | solution.py:312
  65.6 2.0 %copy-start.8 = (s32[1,8]{1,0:T(1,128)S(1)}, s32[1,8]{1,0:T(1,128)}, u32[]{:S(2)}) copy-start(s32[1,8]{1,0:T(1,128)} %mask_ref.1) | copy-start | bytes 100
  65.7 6.3 %collective-permute-start.11 = (bf16[32,2048]{1,0:T(8,128)(2,1)S(1)}, bf16[32,2048]{1,0:T(8,128)(2,1)S(1)}, u32[]{:S(2)}, u32[]{:S(2)}) collective-permute-start(bf16[32,2048]{1,0:T(8,128)(2,1)S(1)} %shard_map.122), channel_id=1, source_target_pairs={{0,4},{4,8},{8,12},{12,16},{16,20},{20,24},{24,28},{1,5},{5,9},{9,... | collective-permute-start | bytes 393224 | tf_op jit(solution)/shard_map/ppermute | solution.py:25

commit v4 on v3

--- a/solution.py
+++ b/solution.py
@@ -68,7 +68,7 @@
     return lax.dot_general(values, tile, (((1,), (1,)), ((), ())), preferred_element_type=F32)
 
 
-def self_kernel(scale, leaf, own_ref, rows_ref, near_ref, norms_ref, tiles_ref):
+def self_kernel(scale, leaf, own_ref, rows_ref, near_ref, norms_ref, tiles_ref, turned_ref):
     dim = own_ref.shape[0] - near_ref.shape[0]
     points_ref, values_ref = own_ref.at[:dim, :], own_ref.at[dim:, :]
     norms_ref[...] = norm_rows(points_ref[...], scale, False)
@@ -82,13 +82,16 @@
             values_ref[:, at[low]], tiles_ref[slot], preferred_element_type=F32
         )
         if low != high:
-            near_ref[:, at[low]] += dot_back(values_ref[:, at[high]], tiles_ref[slot])
+            near_ref[:, at[low]] += jnp.dot(
+                values_ref[:, at[high]], turned_ref[slot], preferred_element_type=F32
+            )
 
     pairs = [(low, high) for low in range(LPD) for high in range(low, LPD)]
     for slot, (low, high) in enumerate(pairs):
-        tiles_ref[slot] = tile_of(
-            rows_ref[at[low], :], points_ref[:, at[high]], norms_ref[:, at[high]]
-        )
+        tile = tile_of(rows_ref[at[low], :], points_ref[:, at[high]], norms_ref[:, at[high]])
+        tiles_ref[slot] = tile
+        if low != high:
+            turned_ref[slot] = tile.T
         if slot:
             add(slot - 1, *pairs[slot - 1])
     add(len(pairs) - 1, *pairs[-1])
@@ -110,6 +113,7 @@
     norms_ref,
     upper_sum,
     tiles_ref,
+    turned_ref,
 ):
     cols = near_ref.shape[0]
     dim = own_ref.shape[0] - cols
@@ -129,19 +133,22 @@
     def add(slot, live, low, high):
         flag = jnp.where(live, 1.0, 0.0).astype(BF16)
         low_at, high_at = pl.ds(low, leaf), pl.ds(high, leaf)
-        tile = tiles_ref[slot]
         upper_sum[:, high_at] += jnp.dot(
-            own_ref[dim:, low_at] * flag, tile, preferred_element_type=F32
+            own_ref[dim:, low_at] * flag, tiles_ref[slot], preferred_element_type=F32
         )
-        near_ref[:, low_at] += dot_back(other_ref[dim:, high_at] * flag, tile)
+        near_ref[:, low_at] += jnp.dot(
+            other_ref[dim:, high_at] * flag, turned_ref[slot], preferred_element_type=F32
+        )
 
     def some_slots(slots):
         for index, (_, low, high) in enumerate(slots):
-            tiles_ref[index] = tile_of(
+            tile = tile_of(
                 rows_ref[pl.ds(low, leaf), :],
                 other_ref[:dim, pl.ds(high, leaf)],
                 norms_ref[:, pl.ds(high, leaf)],
             )
+            tiles_ref[index] = tile
+            turned_ref[index] = tile.T
             if index:
                 add(index - 1, *slots[index - 1])
         add(group - 1, *slots[group - 1])
@@ -240,8 +247,8 @@
             out_ref[...] = ahead_ref[...]
 
 
-def add_kernel(left_ref, right_ref, out_ref):
-    out_ref[...] = (left_ref[...] + right_ref[...]).reshape(out_ref.shape)
+def add_kernel(*refs):
+    refs[-1][0] = functools.reduce(jnp.add, [ref[...] for ref in refs[:-1]])
 
 
 def join_kernel(*refs):
@@ -252,24 +259,11 @@
         start += part.shape[0]
 
 
-def onward_kernel(partners, *refs):
-    row_index = lax.axis_index("gy")
-    total = refs[0][...].astype(F32)
-    for partner, ref in zip(partners, refs[1:-1]):
-        lower_side = (row_index >> (partner.bit_length() - 1)) & 1 == 0
-        total += ref[...].astype(F32) * jnp.where(lower_side, 1.0, 0.0)
-    refs[-1][...] = total.astype(BF16)
-
-
-def fall_kernel(partners, near_ref, root_ref, spread_ref, *refs):
-    row_index = lax.axis_index("gy")
+def fall_kernel(near_ref, root_ref, spread_ref, out_ref):
     total = near_ref[...]
     for part in split3(root_ref[...]):
         total += jnp.dot(part, spread_ref[...], preferred_element_type=F32)
-    for partner, ref in zip(partners, refs[:-1]):
-        upper_side = (row_index >> (partner.bit_length() - 1)) & 1 == 1
-        total += ref[...].astype(F32) * jnp.where(upper_side, 1.0, 0.0)
-    refs[-1][...] = total
+    out_ref[...] = total
 
 
 def last_kernel(local_ref, *refs):
@@ -333,7 +327,7 @@
     gx_count, reach = lax.axis_size("gx"), lax.axis_size("gy")
     levels = reach.bit_length() - 1
     slots = near_lower.shape[2]
-    group = next(size for size in (4, 3, 2, 1) if slots % size == 0)
+    group = next(size for size in range(12, 0, -1) if slots % size == 0)
     tile_flops = 2 * leaf * leaf * (256 + 2 * 256)
     block = kept(dim + cols, device_cols, dtype=BF16)
     root_shape = (dim + cols, SKEL)
@@ -354,10 +348,9 @@
         flops=2**29,
         memory=6,
     )
-    for bit in range(levels):
-        outs = kept(*root_shape) if bit + 1 < levels else kept(1, *root_shape)
-        share = run(add_kernel, outs, share, swapped(share, "gy", 1 << bit))
-    roots, sent = [share], share
+    shares = [swapped(share, "gy", partner) for partner in range(1, reach)]
+    own_root = run(add_kernel, kept(1, *root_shape), share, *shares)
+    roots, sent = [own_root], own_root
     for bit in range(gx_count.bit_length() - 1):
         if bit:
             sent = run(join_kernel, kept(1 << bit, *root_shape), *roots)
@@ -368,9 +361,10 @@
         (kept(device_cols, width, dtype=BF16), kept(cols, device_cols)),
         packed,
         flops=10 * tile_flops,
-        memory=12,
+        memory=20,
         scratch=[
             pltpu.VMEM((ROWS_AUG, device_cols), BF16),
+            pltpu.VMEM((LPD * (LPD + 1) // 2, leaf, leaf), BF16),
             pltpu.VMEM((LPD * (LPD + 1) // 2, leaf, leaf), BF16),
         ],
     )
@@ -386,46 +380,31 @@
             other,
             near,
             flops=slots * tile_flops,
-            memory=10,
+            memory=24,
             scratch=[
                 pltpu.VMEM((ROWS_AUG, device_cols), BF16),
                 pltpu.VMEM((cols, device_cols), F32),
                 pltpu.VMEM((group, leaf, leaf), BF16),
+                pltpu.VMEM((group, leaf, leaf), BF16),
             ],
             aliases={5: 0},
         )
 
     payloads = run(route_kernel, (block,) * levels, packed, ahead)
-    others = [ahead]
-    for partner in range(1, reach):
-        others.append(swapped(payloads[partner.bit_length() - 1], "gy", partner))
-    near, first_upper = meet(0, ahead, near)
-    partners, backs = list(range(1, reach - 1)), []
-    for partner in partners:
+    others = {
+        partner: swapped(payloads[partner.bit_length() - 1], "gy", partner)
+        for partner in range(reach - 1, 0, -1)
+    }
+    near, upper = meet(0, ahead, near)
+    landed = [passed_along(upper, "gx", 1)]
+    for partner in range(reach - 1, 0, -1):
         near, upper = meet(partner, others[partner], near)
-        backs.append(swapped(upper, "gy", partner))
-    near, upper = meet(reach - 1, others[reach - 1], near)
-    direct = landing(reach - 1, upper)
-    onward = run(
-        functools.partial(onward_kernel, partners),
-        kept(cols, device_cols, dtype=BF16),
-        first_upper,
-        *backs,
-    )
-    landed = passed_along(onward, "gx", 1)
+        landed.append(landing(partner, upper))
     root = run(
         functools.partial(root_kernel, scale), kept(cols, SKEL), far_mask, *roots, flops=2**28
     )
-    local = run(
-        functools.partial(fall_kernel, partners),
-        kept(cols, device_cols),
-        near,
-        root,
-        spread,
-        *backs,
-        flops=2**26,
-    )
-    return run(last_kernel, shape(cols, device_cols), local, landed, direct)
+    local = run(fall_kernel, kept(cols, device_cols), near, root, spread, flops=2**26)
+    return run(last_kernel, shape(cols, device_cols), local, *landed)
 
 
 def solution(mesh):

time: 73 us -> 64.5 us (0.88)
  the two profiles are of different devices: /device:TPU:18 before, /device:TPU:5 now
where the time goes in v4:
time: 64.5 us; the launch traced here: 63.4 us
  starting transfers between devices  34.2 us (53%)
  Pallas kernels  21.8 us (34%)
  waiting for transfers between devices  5.38 us (8%)
  local copies, waits for them, and re-layouts  1.72 us (3%)
    pallas_call x13, Pallas kernels, run(): pl.pallas_call(kernel, out_shape=outs, in_specs=[VMEM] * len(args), out_s...  21.8 us
    ppermute x3, starting transfers between devices, landing(): return lax.ppermute(back, ('gx', 'gy'), pairs)  12.2 us
    ppermute x9, starting transfers between devices, swapped(): return lax.ppermute(value, axis, pairs)  11.6 us
    ppermute x2, starting transfers between devices, passed_along(): return lax.ppermute(value, axis, pairs)  10.4 us
    ppermute x9, waiting for transfers between devices, swapped(): return lax.ppermute(value, axis, pairs)  2.67 us
    ppermute x3, waiting for transfers between devices, landing(): return lax.ppermute(back, ('gx', 'gy'), pairs)  1.94 us
    unnamed x21, local copies, waits for them, and re-layouts  1.71 us
  transfers between devices with their start and end apart: 14, of which 5 were waited for; matrix products, arithmetic and copies ran while one was open for 0% of the time, Pallas kernels for 31%

profile of v4, /device:TPU:5, one launch (start us, length us, event | category | flops | bytes accessed | tf_op | source)
XLA Modules:
  0.0 63.4 jit_solution(12714344525695298493)
XLA Ops:
  0.0 1.0 %constant_dynamic-update-slice_fusion.1 = bf16[96,2048]{1,0:T(8,128)(2,1)S(1)} fusion(bf16[64,2048]{1,0:T(8,128)(2,1)} %param.11), kind=kLoop, calls=%fused_computation.1 | loop fusion | bytes 524288
  1.8 1.2 %shard_map.115 = (f32[96,128]{1,0:T(8,128)S(1)}, bf16[128,2048]{1,0:T(8,128)(2,1)S(1)}) custom-call(bf16[96,2048]{1,0:T(8,128)(2,1)S(1)} %constant_dynamic-update-slice_fusion.own_ref, s32[4,128]{1,0:T(4,128)S(1)} %copy-done.2, s32[4,512]{1,0:T(4,128)S(1)} %copy-done, s32[1,128]{1,0:T(1,128)S(1)} %copy-done.7, s32[1,512]{1,0:T(1,128)S(1)} %copy-done.3, ...), custom_call_target="tpu_custom_call" | custom-call | flops 536870912 | bytes 65536 | tf_op jit(solution)/shard_map/pallas_call | solution.py:286
  3.0 1.3 %collective-permute-start.4 = (f32[96,128]{1,0:T(8,128)S(1)}, f32[96,128]{1,0:T(8,128)S(1)}, u32[]{:S(2)}, u32[]{:S(2)}) collective-permute-start(f32[96,128]{1,0:T(8,128)S(1)} %get-tuple-element.27.refs_0_), channel_id=1, source_target_pairs={{0,1},{1,0},{2,3},{3,2},{4,5},{5,4},{6,7},{7,6},{8,9},{9,8},{10,11... | collective-permute-start | bytes 147464 | tf_op jit(solution)/shard_map/ppermute | solution.py:30
  4.5 1.2 %collective-permute-start.6 = (f32[96,128]{1,0:T(8,128)S(1)}, f32[96,128]{1,0:T(8,128)S(1)}, u32[]{:S(2)}, u32[]{:S(2)}) collective-permute-start(f32[96,128]{1,0:T(8,128)S(1)} %get-tuple-element.27.refs_0_), channel_id=1, source_target_pairs={{0,3},{1,2},{2,1},{3,0},{4,7},{5,6},{6,5},{7,4},{8,11},{9,10},{10,... | collective-permute-start | bytes 147464 | tf_op jit(solution)/shard_map/ppermute | solution.py:30
  6.0 1.4 %collective-permute-done.5.refs_2_ = f32[96,128]{1,0:T(8,128)S(1)} collective-permute-done((f32[96,128]{1,0:T(8,128)S(1)}, f32[96,128]{1,0:T(8,128)S(1)}, u32[]{:S(2)}, u32[]{:S(2)}) %collective-permute-start.5) | collective-permute-done | bytes 49184 | tf_op jit(solution)/shard_map/ppermute | solution.py:30
  7.4 0.9 %collective-permute-done.6.refs_3_ = f32[96,128]{1,0:T(8,128)S(1)} collective-permute-done((f32[96,128]{1,0:T(8,128)S(1)}, f32[96,128]{1,0:T(8,128)S(1)}, u32[]{:S(2)}, u32[]{:S(2)}) %collective-permute-start.6) | collective-permute-done | bytes 49184 | tf_op jit(solution)/shard_map/ppermute | solution.py:30
  8.3 2.4 %collective-permute-start.7 = (f32[1,96,128]{2,1,0:T(8,128)S(1)}, f32[1,96,128]{2,1,0:T(8,128)S(1)}, u32[]{:S(2)}, u32[]{:S(2)}) collective-permute-start(f32[1,96,128]{2,1,0:T(8,128)S(1)} %shard_map.116.refs_0_), channel_id=1, source_target_pairs={{0,4},{4,0},{8,12},{12,8},{16,20},{20,16},{24,28},{28,24},{1,5},{5... | collective-permute-start | bytes 147464 | tf_op jit(solution)/shard_map/ppermute | solution.py:30
  10.8 1.9 %collective-permute-start = (bf16[96,2048]{1,0:T(8,128)(2,1)S(1)}, bf16[96,2048]{1,0:T(8,128)(2,1)S(1)}, u32[]{:S(2)}, u32[]{:S(2)}) collective-permute-start(bf16[96,2048]{1,0:T(8,128)(2,1)S(1)} %constant_dynamic-update-slice_fusion.own_ref), channel_id=1, source_target_pairs={{4,0},{8,4},{12,8},{16,12},{20,16},{24,20},{28,24},{5,1},{9,5},{13... | collective-permute-start | bytes 1179656 | tf_op jit(solution)/shard_map/ppermute | solution.py:25
  12.7 1.4 %collective-permute-start.8 = (f32[2,96,128]{2,1,0:T(8,128)S(1)}, f32[2,96,128]{2,1,0:T(8,128)S(1)}, u32[]{:S(2)}, u32[]{:S(2)}) collective-permute-start(f32[2,96,128]{2,1,0:T(8,128)S(1)} %shard_map.117), channel_id=1, source_target_pairs={{0,8},{4,12},{8,0},{12,4},{16,24},{20,28},{24,16},{28,20},{1,9},{5... | collective-permute-start | bytes 294920 | tf_op jit(solution)/shard_map/ppermute | solution.py:30
  14.1 3.2 %shard_map.109 = (bf16[2048,208]{1,0:T(8,128)(2,1)S(1)}, f32[32,2048]{1,0:T(8,128)S(1)}) custom-call(bf16[96,2048]{1,0:T(8,128)(2,1)S(1)} %constant_dynamic-update-slice_fusion.own_ref), custom_call_target="tpu_custom_call" | custom-call | flops 4026531840 | bytes 65536 | tf_op jit(solution)/shard_map/pallas_call | solution.py:286
  17.3 2.4 %collective-permute-start.9 = (f32[4,96,128]{2,1,0:T(8,128)S(1)}, f32[4,96,128]{2,1,0:T(8,128)S(1)}, u32[]{:S(2)}, u32[]{:S(2)}) collective-permute-start(f32[4,96,128]{2,1,0:T(8,128)S(1)} %shard_map.118), channel_id=1, source_target_pairs={{0,16},{4,20},{8,24},{12,28},{16,0},{20,4},{24,8},{28,12},{1,17},{... | collective-permute-start | bytes 589832 | tf_op jit(solution)/shard_map/ppermute | solution.py:30
  20.5 1.3 %collective-permute-start.2 = (bf16[96,2048]{1,0:T(8,128)(2,1)S(1)}, bf16[96,2048]{1,0:T(8,128)(2,1)S(1)}, u32[]{:S(2)}, u32[]{:S(2)}) collective-permute-start(bf16[96,2048]{1,0:T(8,128)(2,1)S(1)} %get-tuple-element.21), channel_id=1, source_target_pairs={{0,2},{1,3},{2,0},{3,1},{4,6},{5,7},{6,4},{7,5},{8,10},{9,11},{10,... | collective-permute-start | bytes 1179656 | tf_op jit(solution)/shard_map/ppermute | solution.py:30
  21.9 1.4 %collective-permute-start.1 = (bf16[96,2048]{1,0:T(8,128)(2,1)S(1)}, bf16[96,2048]{1,0:T(8,128)(2,1)S(1)}, u32[]{:S(2)}, u32[]{:S(2)}) collective-permute-start(bf16[96,2048]{1,0:T(8,128)(2,1)S(1)} %get-tuple-element.20), channel_id=1, source_target_pairs={{0,1},{1,0},{2,3},{3,2},{4,5},{5,4},{6,7},{7,6},{8,9},{9,8},{10,11... | collective-permute-start | bytes 1179656 | tf_op jit(solution)/shard_map/ppermute | solution.py:30
  23.2 3.8 %shard_map.111 = (f32[32,2048]{1,0:T(8,128)S(1)}, bf16[32,2048]{1,0:T(8,128)(2,1)S(1)}) custom-call(s32[1,4,12]{2,1,0:T(4,128)S(1)} %copy-done.4, s32[1,4,12]{2,1,0:T(4,128)S(1)} %copy-done.5, bf16[2048,208]{1,0:T(8,128)(2,1)S(1)} %get-tuple-element.19.rows_ref, ...), custom_call_target="tpu_custom_call", output_to_operand_aliasing={{0}: (5, {})} | custom-call | flops 4831838208 | bytes 65536 | tf_op jit(solution)/shard_map/pallas_call | solution.py:286
  27.1 8.4 %collective-permute-start.10 = (bf16[32,2048]{1,0:T(8,128)(2,1)S(1)}, bf16[32,2048]{1,0:T(8,128)(2,1)S(1)}, u32[]{:S(2)}, u32[]{:S(2)}) collective-permute-start(bf16[32,2048]{1,0:T(8,128)(2,1)S(1)} %get-tuple-element.29), channel_id=1, source_target_pairs={{0,4},{4,8},{8,12},{12,16},{16,20},{20,24},{24,28},{1,5},{5,9},{9,... | collective-permute-start | bytes 393224 | tf_op jit(solution)/shard_map/ppermute | solution.py:25
  35.5 3.8 %shard_map.112 = (f32[32,2048]{1,0:T(8,128)S(1)}, bf16[32,2048]{1,0:T(8,128)(2,1)S(1)}) custom-call(s32[1,4,12]{2,1,0:T(4,128)S(1)} %copy-done.4, s32[1,4,12]{2,1,0:T(4,128)S(1)} %copy-done.5, bf16[2048,208]{1,0:T(8,128)(2,1)S(1)} %get-tuple-element.19.rows_ref, ...), custom_call_target="tpu_custom_call", output_to_operand_aliasing={{0}: (5, {})} | custom-call | flops 4831838208 | bytes 65536 | tf_op jit(solution)/shard_map/pallas_call | solution.py:286
  39.3 5.7 %collective-permute-start.11 = (bf16[32,2048]{1,0:T(8,128)(2,1)S(1)}, bf16[32,2048]{1,0:T(8,128)(2,1)S(1)}, u32[]{:S(2)}, u32[]{:S(2)}) collective-permute-start(bf16[32,2048]{1,0:T(8,128)(2,1)S(1)} %get-tuple-element.30), channel_id=1, source_target_pairs={{0,3},{1,2},{2,5},{3,4},{4,7},{5,6},{6,9},{7,8},{8,11},{9,10},{10,... | collective-permute-start | bytes 393224 | tf_op jit(solution)/shard_map/ppermute | solution.py:306
  45.0 4.0 %shard_map.113 = (f32[32,2048]{1,0:T(8,128)S(1)}, bf16[32,2048]{1,0:T(8,128)(2,1)S(1)}) custom-call(s32[1,4,12]{2,1,0:T(4,128)S(1)} %copy-done.4, s32[1,4,12]{2,1,0:T(4,128)S(1)} %copy-done.5, bf16[2048,208]{1,0:T(8,128)(2,1)S(1)} %get-tuple-element.19.rows_ref, ...), custom_call_target="tpu_custom_call", output_to_operand_aliasing={{0}: (5, {})} | custom-call | flops 4831838208 | bytes 65536 | tf_op jit(solution)/shard_map/pallas_call | solution.py:286
  49.0 3.4 %collective-permute-start.12 = (bf16[32,2048]{1,0:T(8,128)(2,1)S(1)}, bf16[32,2048]{1,0:T(8,128)(2,1)S(1)}, u32[]{:S(2)}, u32[]{:S(2)}) collective-permute-start(bf16[32,2048]{1,0:T(8,128)(2,1)S(1)} %get-tuple-element.31), channel_id=1, source_target_pairs={{0,2},{1,3},{2,4},{3,5},{4,6},{5,7},{6,8},{7,9},{8,10},{9,11},{10,... | collective-permute-start | bytes 393224 | tf_op jit(solution)/shard_map/ppermute | solution.py:306
  52.5 3.8 %shard_map.114 = (f32[32,2048]{1,0:T(8,128)S(1)}, bf16[32,2048]{1,0:T(8,128)(2,1)S(1)}) custom-call(s32[1,4,12]{2,1,0:T(4,128)S(1)} %copy-done.4, s32[1,4,12]{2,1,0:T(4,128)S(1)} %copy-done.5, bf16[2048,208]{1,0:T(8,128)(2,1)S(1)} %get-tuple-element.19.rows_ref, ...), custom_call_target="tpu_custom_call", output_to_operand_aliasing={{0}: (5, {})} | custom-call | flops 4831838208 | bytes 65536 | tf_op jit(solution)/shard_map/pallas_call | solution.py:286
  56.3 3.1 %collective-permute-start.13 = (bf16[32,2048]{1,0:T(8,128)(2,1)S(1)}, bf16[32,2048]{1,0:T(8,128)(2,1)S(1)}, u32[]{:S(2)}, u32[]{:S(2)}) collective-permute-start(bf16[32,2048]{1,0:T(8,128)(2,1)S(1)} %get-tuple-element.32), channel_id=1, source_target_pairs={{0,1},{1,4},{2,3},{3,6},{4,5},{5,8},{6,7},{7,10},{8,9},{9,12},{10,... | collective-permute-start | bytes 393224 | tf_op jit(solution)/shard_map/ppermute | solution.py:306
  59.5 0.8 %shard_map.119.root_ref = f32[32,128]{1,0:T(8,128)S(1)} custom-call(s32[1,8]{1,0:T(1,128)S(1)} %copy-done.8, f32[1,96,128]{2,1,0:T(8,128)S(1)} %shard_map.116.refs_0_, f32[1,96,128]{2,1,0:T(8,128)S(1)} %collective-permute-done.7.refs_1_, f32[2,96,128]{2,1,0:T(8,128)S(1)} %collective-permute-done.8.refs_2_, f32[4,96,128]{2,1,0:T(8,128)S(1)} %collective-permute-done.9.refs_3_), custom_call_target="tpu_custom_call" | custom-call | flops 268435456 | bytes 65536 | tf_op jit(solution)/shard_map/pallas_call | solution.py:286
  60.7 1.9 %collective-permute-done.13.refs_3_ = bf16[32,2048]{1,0:T(8,128)(2,1)S(1)} collective-permute-done((bf16[32,2048]{1,0:T(8,128)(2,1)S(1)}, bf16[32,2048]{1,0:T(8,128)(2,1)S(1)}, u32[]{:S(2)}, u32[]{:S(2)}) %collective-permute-start.13) | collective-permute-done | bytes 131104 | tf_op jit(solution)/shard_map/ppermute | solution.py:306
  62.6 0.8 %shard_map.121 = f32[32,2048]{1,0:T(8,128)} custom-call(f32[32,2048]{1,0:T(8,128)S(1)} %shard_map.120.local_ref, bf16[32,2048]{1,0:T(8,128)(2,1)S(1)} %collective-permute-done.10.refs_0_, bf16[32,2048]{1,0:T(8,128)(2,1)S(1)} %collective-permute-done.11.refs_1_, bf16[32,2048]{1,0:T(8,128)(2,1)S(1)} %collective-permute-done.12.refs_2_, ...), custom_call_target="tpu_custom_call" | custom-call | flops 1048576 | bytes 65536 | tf_op jit(solution)/shard_map/pallas_call | solution.py:286
  (39 shorter events, 2.5 us)
Async XLA Ops:
  0.0 1.0 %copy-start.9 = (bf16[32,2048]{1,0:T(8,128)(2,1)S(1)}, bf16[32,2048]{1,0:T(8,128)(2,1)}, u32[]{:S(2)}) copy-start(bf16[32,2048]{1,0:T(8,128)(2,1)} %param.12) | copy-start | bytes 393220
  1.0 0.7 %copy-start = (s32[4,512]{1,0:T(4,128)S(1)}, s32[4,512]{1,0:T(4,128)}, u32[]{:S(2)}) copy-start(s32[4,512]{1,0:T(4,128)} %leaf_assign.1) | copy-start | bytes 24580
  1.0 0.7 %copy-start.2 = (s32[4,128]{1,0:T(4,128)S(1)}, s32[4,128]{1,0:T(4,128)}, u32[]{:S(2)}) copy-start(s32[4,128]{1,0:T(4,128)} %leaf_pick.1) | copy-start | bytes 6148
  1.0 0.7 %copy-start.3 = (s32[1,512]{1,0:T(1,128)S(1)}, s32[1,512]{1,0:T(1,128)}, u32[]{:S(2)}) copy-start(s32[1,512]{1,0:T(1,128)} %device_assign.1) | copy-start | bytes 6148
  1.1 0.7 %copy-start.6 = (s32[1,3,128]{2,0,1:T(1,128)S(1)}, s32[1,3,128]{2,0,1:T(1,128)}, u32[]{:S(2)}) copy-start(s32[1,3,128]{2,0,1:T(1,128)} %param.17) | copy-start | bytes 4612
  1.1 0.7 %copy-start.1 = (s32[1,3,256]{2,0,1:T(1,128)S(1)}, s32[1,3,256]{2,0,1:T(1,128)}, u32[]{:S(2)}) copy-start(s32[1,3,256]{2,0,1:T(1,128)} %param.18) | copy-start | bytes 9220
  1.1 0.7 %copy-start.7 = (s32[1,128]{1,0:T(1,128)S(1)}, s32[1,128]{1,0:T(1,128)}, u32[]{:S(2)}) copy-start(s32[1,128]{1,0:T(1,128)} %device_pick.1) | copy-start | bytes 1540
  3.0 3.0 %collective-permute-start.4 = (f32[96,128]{1,0:T(8,128)S(1)}, f32[96,128]{1,0:T(8,128)S(1)}, u32[]{:S(2)}, u32[]{:S(2)}) collective-permute-start(f32[96,128]{1,0:T(8,128)S(1)} %get-tuple-element.27.refs_0_), channel_id=1, source_target_pairs={{0,1},{1,0},{2,3},{3,2},{4,5},{5,4},{6,7},{7,6},{8,9},{9,8},{10,11... | collective-permute-start | bytes 147464 | tf_op jit(solution)/shard_map/ppermute | solution.py:30
  4.2 3.2 %collective-permute-start.5 = (f32[96,128]{1,0:T(8,128)S(1)}, f32[96,128]{1,0:T(8,128)S(1)}, u32[]{:S(2)}, u32[]{:S(2)}) collective-permute-start(f32[96,128]{1,0:T(8,128)S(1)} %get-tuple-element.27.refs_0_), channel_id=1, source_target_pairs={{0,2},{1,3},{2,0},{3,1},{4,6},{5,7},{6,4},{7,5},{8,10},{9,11},{10,... | collective-permute-start | bytes 147464 | tf_op jit(solution)/shard_map/ppermute | solution.py:30
  4.5 3.9 %collective-permute-start.6 = (f32[96,128]{1,0:T(8,128)S(1)}, f32[96,128]{1,0:T(8,128)S(1)}, u32[]{:S(2)}, u32[]{:S(2)}) collective-permute-start(f32[96,128]{1,0:T(8,128)S(1)} %get-tuple-element.27.refs_0_), channel_id=1, source_target_pairs={{0,3},{1,2},{2,1},{3,0},{4,7},{5,6},{6,5},{7,4},{8,11},{9,10},{10,... | collective-permute-start | bytes 147464 | tf_op jit(solution)/shard_map/ppermute | solution.py:30
  8.3 4.4 %collective-permute-start.7 = (f32[1,96,128]{2,1,0:T(8,128)S(1)}, f32[1,96,128]{2,1,0:T(8,128)S(1)}, u32[]{:S(2)}, u32[]{:S(2)}) collective-permute-start(f32[1,96,128]{2,1,0:T(8,128)S(1)} %shard_map.116.refs_0_), channel_id=1, source_target_pairs={{0,4},{4,0},{8,12},{12,8},{16,20},{20,16},{24,28},{28,24},{1,5},{5... | collective-permute-start | bytes 147464 | tf_op jit(solution)/shard_map/ppermute | solution.py:30
  10.8 9.7 %collective-permute-start = (bf16[96,2048]{1,0:T(8,128)(2,1)S(1)}, bf16[96,2048]{1,0:T(8,128)(2,1)S(1)}, u32[]{:S(2)}, u32[]{:S(2)}) collective-permute-start(bf16[96,2048]{1,0:T(8,128)(2,1)S(1)} %constant_dynamic-update-slice_fusion.own_ref), channel_id=1, source_target_pairs={{4,0},{8,4},{12,8},{16,12},{20,16},{24,20},{28,24},{5,1},{9,5},{13... | collective-permute-start | bytes 1179656 | tf_op jit(solution)/shard_map/ppermute | solution.py:25
  12.7 4.5 %collective-permute-start.8 = (f32[2,96,128]{2,1,0:T(8,128)S(1)}, f32[2,96,128]{2,1,0:T(8,128)S(1)}, u32[]{:S(2)}, u32[]{:S(2)}) collective-permute-start(f32[2,96,128]{2,1,0:T(8,128)S(1)} %shard_map.117), channel_id=1, source_target_pairs={{0,8},{4,12},{8,0},{12,4},{16,24},{20,28},{24,16},{28,20},{1,9},{5... | collective-permute-start | bytes 294920 | tf_op jit(solution)/shard_map/ppermute | solution.py:30
  17.3 42.1 %collective-permute-start.9 = (f32[4,96,128]{2,1,0:T(8,128)S(1)}, f32[4,96,128]{2,1,0:T(8,128)S(1)}, u32[]{:S(2)}, u32[]{:S(2)}) collective-permute-start(f32[4,96,128]{2,1,0:T(8,128)S(1)} %shard_map.118), channel_id=1, source_target_pairs={{0,16},{4,20},{8,24},{12,28},{16,0},{20,4},{24,8},{28,12},{1,17},{... | collective-permute-start | bytes 589832 | tf_op jit(solution)/shard_map/ppermute | solution.py:30
  20.5 24.5 %collective-permute-start.2 = (bf16[96,2048]{1,0:T(8,128)(2,1)S(1)}, bf16[96,2048]{1,0:T(8,128)(2,1)S(1)}, u32[]{:S(2)}, u32[]{:S(2)}) collective-permute-start(bf16[96,2048]{1,0:T(8,128)(2,1)S(1)} %get-tuple-element.21), channel_id=1, source_target_pairs={{0,2},{1,3},{2,0},{3,1},{4,6},{5,7},{6,4},{7,5},{8,10},{9,11},{10,... | collective-permute-start | bytes 1179656 | tf_op jit(solution)/shard_map/ppermute | solution.py:30
  21.8 13.7 %collective-permute-start.3 = (bf16[96,2048]{1,0:T(8,128)(2,1)S(1)}, bf16[96,2048]{1,0:T(8,128)(2,1)S(1)}, u32[]{:S(2)}, u32[]{:S(2)}) collective-permute-start(bf16[96,2048]{1,0:T(8,128)(2,1)S(1)} %get-tuple-element.21), channel_id=1, source_target_pairs={{0,3},{1,2},{2,1},{3,0},{4,7},{5,6},{6,5},{7,4},{8,11},{9,10},{10,... | collective-permute-start | bytes 1179656 | tf_op jit(solution)/shard_map/ppermute | solution.py:30
  21.9 1.4 %copy-start.5 = (s32[1,4,12]{2,1,0:T(4,128)S(1)}, s32[1,4,12]{2,1,0:T(4,128)}, u32[]{:S(2)}) copy-start(s32[1,4,12]{2,1,0:T(4,128)} %upper_ref.7) | copy-start | bytes 580
  21.9 1.4 %copy-start.4 = (s32[1,4,12]{2,1,0:T(4,128)S(1)}, s32[1,4,12]{2,1,0:T(4,128)}, u32[]{:S(2)}) copy-start(s32[1,4,12]{2,1,0:T(4,128)} %lower_ref.7) | copy-start | bytes 580
  21.9 30.6 %collective-permute-start.1 = (bf16[96,2048]{1,0:T(8,128)(2,1)S(1)}, bf16[96,2048]{1,0:T(8,128)(2,1)S(1)}, u32[]{:S(2)}, u32[]{:S(2)}) collective-permute-start(bf16[96,2048]{1,0:T(8,128)(2,1)S(1)} %get-tuple-element.20), channel_id=1, source_target_pairs={{0,1},{1,0},{2,3},{3,2},{4,5},{5,4},{6,7},{7,6},{8,9},{9,8},{10,11... | collective-permute-start | bytes 1179656 | tf_op jit(solution)/shard_map/ppermute | solution.py:30
  27.1 33.6 %collective-permute-start.10 = (bf16[32,2048]{1,0:T(8,128)(2,1)S(1)}, bf16[32,2048]{1,0:T(8,128)(2,1)S(1)}, u32[]{:S(2)}, u32[]{:S(2)}) collective-permute-start(bf16[32,2048]{1,0:T(8,128)(2,1)S(1)} %get-tuple-element.29), channel_id=1, source_target_pairs={{0,4},{4,8},{8,12},{12,16},{16,20},{20,24},{24,28},{1,5},{5,9},{9,... | collective-permute-start | bytes 393224 | tf_op jit(solution)/shard_map/ppermute | solution.py:25
  39.3 21.3 %collective-permute-start.11 = (bf16[32,2048]{1,0:T(8,128)(2,1)S(1)}, bf16[32,2048]{1,0:T(8,128)(2,1)S(1)}, u32[]{:S(2)}, u32[]{:S(2)}) collective-permute-start(bf16[32,2048]{1,0:T(8,128)(2,1)S(1)} %get-tuple-element.30), channel_id=1, source_target_pairs={{0,3},{1,2},{2,5},{3,4},{4,7},{5,6},{6,9},{7,8},{8,11},{9,10},{10,... | collective-permute-start | bytes 393224 | tf_op jit(solution)/shard_map/ppermute | solution.py:306
  49.0 11.6 %collective-permute-start.12 = (bf16[32,2048]{1,0:T(8,128)(2,1)S(1)}, bf16[32,2048]{1,0:T(8,128)(2,1)S(1)}, u32[]{:S(2)}, u32[]{:S(2)}) collective-permute-start(bf16[32,2048]{1,0:T(8,128)(2,1)S(1)} %get-tuple-element.31), channel_id=1, source_target_pairs={{0,2},{1,3},{2,4},{3,5},{4,6},{5,7},{6,8},{7,9},{8,10},{9,11},{10,... | collective-permute-start | bytes 393224 | tf_op jit(solution)/shard_map/ppermute | solution.py:306
  56.3 3.1 %copy-start.8 = (s32[1,8]{1,0:T(1,128)S(1)}, s32[1,8]{1,0:T(1,128)}, u32[]{:S(2)}) copy-start(s32[1,8]{1,0:T(1,128)} %mask_ref.1) | copy-start | bytes 100
  56.3 6.3 %collective-permute-start.13 = (bf16[32,2048]{1,0:T(8,128)(2,1)S(1)}, bf16[32,2048]{1,0:T(8,128)(2,1)S(1)}, u32[]{:S(2)}, u32[]{:S(2)}) collective-permute-start(bf16[32,2048]{1,0:T(8,128)(2,1)S(1)} %get-tuple-element.32), channel_id=1, source_target_pairs={{0,1},{1,4},{2,3},{3,6},{4,5},{5,8},{6,7},{7,10},{8,9},{9,12},{10,... | collective-permute-start | bytes 393224 | tf_op jit(solution)/shard_map/ppermute | solution.py:306
